TPU v7x, 32 devices: a whole 2x2x4 slice. The times are simulated.
32 devices in a mesh: seq: 4 (over x, core), rep: 8 (over z, y).
Axes of the slice: x: 2, y: 2, z: 4, core: 2. Of those that a mesh axis runs over, the one named last changes fastest.
Arguments:
- x_words: float32 [8, 1024, 768], P('rep', 'seq'), may hold values from -6 to 6
- x_ents: float32 [8, 128, 768], P('rep', 'seq'), may hold values from -6 to 6
- spans: int32 [8, 128, 2], P('rep', 'seq'), may hold values from 0 to 1023, as said below
- word_mask: int32 [8, 1024], P('rep', 'seq'), may hold values 0 or 1
- ent_mask: int32 [8, 128], P('rep', 'seq'), may hold values 0 or 1
- cot_words: float32 [8, 1024, 768], P('rep', 'seq'), may hold values from -6 to 6
- cot_ents: float32 [8, 128, 768], P('rep', 'seq'), may hold values from -6 to 6
- attn_w: float32 [7, 768, 768], P(None, 'seq', 'rep')
- up_w: float32 [768, 3072], P('seq', 'rep'), may hold values from -0.21875 to 0.21875
- down_w: float32 [3072, 768], P('seq', 'rep'), may hold values from -0.109375 to 0.109375
- vecs: float32 [15, 768], replicated
- mom_attn: float32 [7, 768, 768], P(None, 'seq', 'rep'), may hold values from -1.75 to 1.75
- mom_up: float32 [768, 3072], P('seq', 'rep'), may hold values from -5 to 5
- mom_down: float32 [3072, 768], P('seq', 'rep'), may hold values from -5 to 5
- mom_vecs: float32 [15, 768], replicated, may hold values from -64 to 64
- err_attn: float32 [8, 7, 768, 768], P('rep', None, 'seq'), may hold values from -20 to 20
- err_up: float32 [8, 768, 3072], P('rep', 'seq'), may hold values from -64 to 64
- err_down: float32 [8, 3072, 768], P('rep', 'seq'), may hold values from -64 to 64
- attention_prior_right: float32 [7, 768, 8], replicated, may hold values from -6 to 6
- qf_up: float32 [3072, 8], replicated, may hold values from -6 to 6
- qf_down: float32 [768, 8], replicated, may hold values from -6 to 6
Outputs:
- out_words: float32 [8, 1024, 768], P('rep', 'seq')
- out_ents: float32 [8, 128, 768], P('rep', 'seq')
- grad_words: float32 [8, 1024, 768], P('rep', 'seq')
- grad_ents: float32 [8, 128, 768], P('rep', 'seq')
- new_attn: float32 [7, 768, 768], P(None, 'seq', 'rep')
- new_up: float32 [768, 3072], P('seq', 'rep')
- new_down: float32 [3072, 768], P('seq', 'rep')
- new_vecs: float32 [15, 768], replicated
- next_mom_attn: float32 [7, 768, 768], P(None, 'seq', 'rep')
- next_mom_up: float32 [768, 3072], P('seq', 'rep')
- next_mom_down: float32 [3072, 768], P('seq', 'rep')
- next_mom_vecs: float32 [15, 768], replicated
- next_err_attn: float32 [8, 7, 768, 768], P('rep', None, 'seq')
- next_err_up: float32 [8, 768, 3072], P('rep', 'seq')
- next_err_down: float32 [8, 3072, 768], P('rep', 'seq')
- p_attn: float32 [7, 768, 8], P(None, 'seq')
- p_up: float32 [768, 8], P('seq')
- p_down: float32 [3072, 8], P('seq')
- q_attn: float32 [7, 768, 8], replicated
- q_up: float32 [3072, 8], replicated
- q_down: float32 [768, 8], replicated
Inputs may be any that keep to these rules, and one draw needn't show every extreme that they name: spans[b, e, 0] and spans[b, e, 1] are the first and last word of entity e of sequence b; a span holds 1 to 16 words.
All inputs are finite; a program needn't handle non-finite values. No bound on the sum of `word_mask` or of `ent_mask` on one device may be relied on, other than what follows from the above.
Results may differ from a plain program's by a relative error of at most 0.025.
The roundings to bfloat16 on the way count: a program that leaves them out, or rounds other values in their place, can miss the bound.
Values may be sent and summed in bfloat16 or wider, within the bound.
No kernel may reach another device: no remote copies, remote signals or barrier semaphores. Data moves between devices by JAX's collectives and lax.ppermute only.
A program may use at most 192 MiB of HBM per device.

v0:
```python
import math

import jax
import jax.numpy as jnp
from jax import lax
from jax.sharding import PartitionSpec as P

HEADS = 12
WORDS = 1024
ENTS = 128
SPAN = 16
SEQS = 1


HIGH_PRECISION = lax.Precision.HIGHEST
EPS = 1e-05
MASK_FILL = 30000.0
MOMENTUM = 0.9


def span_mean(spans, model_width):
    starts = spans[..., 0]
    finals = spans[..., 1]
    lengths = (finals - starts + 1).astype(jnp.float32)
    offsets = jnp.arange(SPAN, dtype=jnp.int32)
    places = (starts[..., None] + offsets).astype(jnp.float32)
    shares = (offsets <= (finals - starts)[..., None]).astype(jnp.float32) / lengths[..., None]
    half_width = model_width // 2
    rates = jnp.exp(
        jnp.arange(half_width).astype(jnp.float32) * (-2.0 * math.log(10000.0) / model_width)
    )
    angles = places[..., None] * rates
    table = jnp.concatenate([jnp.sin(angles), jnp.cos(angles)], -1)
    return jnp.sum(table * shares[..., None], axis=-2)


def layer_norm(hidden, gain, shift):
    center = hidden - jnp.mean(hidden, -1, keepdims=True)
    rstd = lax.rsqrt(jnp.mean(center * center, -1, keepdims=True) + EPS)
    normed = center * rstd
    return (normed * gain + shift, normed, rstd)


def norm_back(grad, normed, rstd, gain):
    dnormed = grad * gain
    grad_in = rstd * (
        dnormed
        - jnp.mean(dnormed, -1, keepdims=True)
        - normed * jnp.mean(dnormed * normed, -1, keepdims=True)
    )
    return (grad_in, jnp.sum(grad * normed, axis=(0, 1)), jnp.sum(grad, axis=(0, 1)))


def gelu_exact(value):
    return jax.nn.gelu(value, approximate=False)


def project(row_entries, weight_matrix):
    return jnp.einsum("thq,qo->tho", row_entries, weight_matrix, preferred_element_type=jnp.float32)


def project_back(row_entries, weight_matrix):
    return jnp.einsum("hpf,zf->hpz", row_entries, weight_matrix, preferred_element_type=jnp.float32)


def weight_grad(input_arrays, gradient_list):
    return jnp.einsum(
        "cev,ceg->vg", input_arrays, gradient_list, preferred_element_type=jnp.float32
    )


def split_keys(pieces, words_dev, ents_dev, head_count):
    key_piece, live_piece = pieces
    batch_rows = key_piece.shape[0]
    both = key_piece.shape[2]
    model_width = both // 2
    head_dim = model_width // head_count
    rows_dev = words_dev + ents_dev
    blocks = key_piece.shape[1] // rows_dev
    grouped = key_piece.reshape(batch_rows, blocks, rows_dev, both)
    live_grouped = live_piece.reshape(batch_rows, blocks, rows_dev)
    word_part = grouped[:, :, :words_dev].reshape(batch_rows, blocks * words_dev, both)
    ent_part = grouped[:, :, words_dev:].reshape(batch_rows, blocks * ents_dev, both)
    keys_word = word_part[..., :model_width].reshape(batch_rows, -1, head_count, head_dim)
    keys_ent = ent_part[..., :model_width].reshape(batch_rows, -1, head_count, head_dim)
    values = jnp.concatenate(
        [word_part[..., model_width:], ent_part[..., model_width:]], 1
    ).reshape(batch_rows, -1, head_count, head_dim)
    live = jnp.concatenate(
        [
            live_grouped[:, :, :words_dev].reshape(batch_rows, -1),
            live_grouped[:, :, words_dev:].reshape(batch_rows, -1),
        ],
        1,
    )
    offsets = (live.astype(jnp.float32) - 1.0) * MASK_FILL
    return (keys_word, keys_ent, values, offsets, blocks)


def score_block(query_word, query_ent, keys_word, keys_ent, offsets):
    score_word = jnp.einsum(
        "sqhd,skhd->shqk", query_word, keys_word, preferred_element_type=jnp.float32
    )
    score_ent = jnp.einsum(
        "sqhd,skhd->shqk", query_ent, keys_ent, preferred_element_type=jnp.float32
    )
    return jnp.concatenate([score_word, score_ent], -1) + offsets[:, None, None, :]


def flat_heads(array):
    return array.reshape(array.shape[0], array.shape[1], -1)


def join_rows(grad_keys_word, grad_keys_ent, grad_values, blocks, words_dev, ents_dev):
    batch_rows = grad_keys_word.shape[0]
    word_count = grad_keys_word.shape[1]
    word_rows = jnp.concatenate(
        [flat_heads(grad_keys_word), flat_heads(grad_values[:, :word_count])], -1
    )
    ent_rows = jnp.concatenate(
        [flat_heads(grad_keys_ent), flat_heads(grad_values[:, word_count:])], -1
    )
    word_rows = word_rows.reshape(batch_rows, blocks, words_dev, -1)
    ent_rows = ent_rows.reshape(batch_rows, blocks, ents_dev, -1)
    return jnp.concatenate([word_rows, ent_rows], 2).reshape(
        batch_rows, blocks * (words_dev + ents_dev), -1
    )


def from_gram(left, gram):
    lower = jnp.linalg.cholesky(gram)
    return jax.scipy.linalg.solve_triangular(lower, left.T, lower=True).T


def orthonormal(left):
    return from_gram(left, jnp.dot(left.T, left, precision=HIGH_PRECISION))


def on_device(
    x_words,
    x_ents,
    spans,
    word_mask,
    ent_mask,
    cot_words,
    cot_ents,
    attn_w,
    up_w,
    down_w,
    vecs,
    mom_attn,
    mom_up,
    mom_down,
    mom_vecs,
    err_attn,
    err_up,
    err_down,
    attention_prior_right,
    qf_up,
    qf_down,
):
    batch_rows, words_dev, model_width = x_words.shape
    ents_dev = x_ents.shape[1]
    rows_dev = words_dev + ents_dev
    head_count = HEADS
    head_dim = model_width // head_count
    hidden_width = up_w.shape[1] * lax.axis_size("rep")
    seq_count = lax.axis_size("seq")
    rep_count = lax.axis_size("rep")
    seq_index = lax.axis_index("seq")
    rep_index = lax.axis_index("rep")
    lowered = jnp.bfloat16
    column_parts = (
        lax.all_gather(attn_w.astype(lowered), "rep", axis=2, tiled=True),
        lax.all_gather(up_w.astype(lowered), "rep", axis=1, tiled=True),
        lax.all_gather(down_w.astype(lowered), "rep", axis=1, tiled=True),
    )
    w_attn, w_up, w_down = (
        lax.all_gather(column_parts[0], "seq", axis=1, tiled=True),
        lax.all_gather(column_parts[1], "seq", axis=0, tiled=True),
        lax.all_gather(column_parts[2], "seq", axis=0, tiled=True),
    )
    input_arrays = jnp.concatenate([x_words, x_ents + span_mean(spans, model_width)], 1)
    inputs_low = input_arrays.astype(lowered)
    word_low = inputs_low[:, :words_dev]
    ent_low = inputs_low[:, words_dev:]
    query_word = (
        jnp.concatenate(
            [project(word_low, w_attn[0]) + vecs[0], project(ent_low, w_attn[2]) + vecs[2]], 1
        )
        * 0.125
    ).astype(lowered)
    query_ent = (
        jnp.concatenate(
            [project(word_low, w_attn[1]) + vecs[1], project(ent_low, w_attn[3]) + vecs[3]], 1
        )
        * 0.125
    ).astype(lowered)
    keys_low = project(inputs_low, w_attn[4]).astype(lowered)
    values_low = (project(inputs_low, w_attn[5]) + vecs[4]).astype(lowered)
    key_rows = jnp.concatenate([keys_low, values_low], -1)
    key_live = jnp.concatenate([word_mask, ent_mask], 1).astype(lowered)
    heads_word = query_word.reshape(batch_rows, rows_dev, head_count, head_dim)
    heads_ent = query_ent.reshape(batch_rows, rows_dev, head_count, head_dim)
    forward_row_top = jnp.full((batch_rows, head_count, rows_dev), -jnp.inf, jnp.float32)
    row_total = jnp.zeros((batch_rows, head_count, rows_dev), jnp.float32)
    weighted = jnp.zeros((batch_rows, rows_dev, head_count, head_dim), jnp.float32)
    keys_word, keys_ent, values, offsets, blocks = split_keys(
        (
            lax.all_gather(key_rows, "seq", axis=1, tiled=True),
            lax.all_gather(key_live, "seq", axis=1, tiled=True),
        ),
        words_dev,
        ents_dev,
        head_count,
    )
    scores = score_block(heads_word, heads_ent, keys_word, keys_ent, offsets)
    new_top = jnp.max(scores, -1)
    factor = jnp.exp(forward_row_top - new_top)
    weights = jnp.exp(scores - new_top[..., None])
    row_total = row_total * factor + jnp.sum(weights, -1)
    weighted = weighted * jnp.transpose(factor, (0, 2, 1))[..., None] + jnp.einsum(
        "shqk,skhd->sqhd", weights.astype(lowered), values, preferred_element_type=jnp.float32
    )
    row_top, row_total, weighted = (new_top, row_total, weighted)
    total_rows = jnp.transpose(row_total, (0, 2, 1))[..., None]
    attn = weighted / total_rows
    attn_low = attn.reshape(batch_rows, rows_dev, model_width).astype(lowered)
    branch = project(attn_low, w_attn[6]) + vecs[5]
    mid, normed_one, rstd_one = layer_norm(input_arrays + branch, vecs[7], vecs[8])
    mid_low = mid.astype(lowered)
    pre = project(mid_low, w_up) + vecs[11:15].reshape(hidden_width)
    act_low = gelu_exact(pre).astype(lowered)
    ffn = project(act_low, w_down) + vecs[6]
    result, normed_two, rstd_two = layer_norm(mid + ffn, vecs[9], vecs[10])
    grad_result = jnp.concatenate([cot_words, cot_ents], 1)
    grad_two, gain_two, shift_two = norm_back(grad_result, normed_two, rstd_two, vecs[9])
    bias_down = jnp.sum(grad_two, axis=(0, 1))
    grad_ffn_low = grad_two.astype(lowered)
    grad_down = weight_grad(act_low, grad_ffn_low)
    grad_act = project_back(grad_ffn_low, w_down)
    unused_value, gelu_pull = jax.vjp(gelu_exact, pre)
    grad_pre = gelu_pull(grad_act)[0]
    bias_up = jnp.sum(grad_pre, axis=(0, 1))
    grad_pre_low = grad_pre.astype(lowered)
    grad_up = weight_grad(mid_low, grad_pre_low)
    grad_mid = grad_two + project_back(grad_pre_low, w_up)
    grad_one, gain_one, shift_one = norm_back(grad_mid, normed_one, rstd_one, vecs[7])
    bias_out = jnp.sum(grad_one, axis=(0, 1))
    grad_branch_low = grad_one.astype(lowered)
    grad_out_proj = weight_grad(attn_low, grad_branch_low)
    grad_attn = project_back(grad_branch_low, w_attn[6]).reshape(
        batch_rows, rows_dev, head_count, head_dim
    )
    grad_unnorm = (grad_attn / total_rows).astype(lowered)
    delta_rows = jnp.transpose(jnp.sum(grad_attn * attn, -1), (0, 2, 1)) / row_total
    keys_word, keys_ent, values, offsets, blocks = split_keys(
        (
            lax.all_gather(key_rows, "seq", axis=1, tiled=True),
            lax.all_gather(key_live, "seq", axis=1, tiled=True),
        ),
        words_dev,
        ents_dev,
        head_count,
    )
    scores = score_block(heads_word, heads_ent, keys_word, keys_ent, offsets)
    weights = jnp.exp(scores - row_top[..., None])
    grad_weights = jnp.einsum(
        "sqhd,skhd->shqk", grad_unnorm, values, preferred_element_type=jnp.float32
    )
    grad_scores = (weights * (grad_weights - delta_rows[..., None])).astype(lowered)
    word_count = keys_word.shape[1]
    scores_word = grad_scores[..., :word_count]
    scores_ent = grad_scores[..., word_count:]
    grad_query_word = jnp.einsum(
        "shqk,skhd->sqhd", scores_word, keys_word, preferred_element_type=jnp.float32
    )
    grad_query_ent = jnp.einsum(
        "shqk,skhd->sqhd", scores_ent, keys_ent, preferred_element_type=jnp.float32
    )
    grad_keys_word = jnp.einsum(
        "shqk,sqhd->skhd", scores_word, heads_word, preferred_element_type=jnp.float32
    )
    grad_keys_ent = jnp.einsum(
        "shqk,sqhd->skhd", scores_ent, heads_ent, preferred_element_type=jnp.float32
    )
    grad_values = jnp.einsum(
        "shqk,sqhd->skhd", weights.astype(lowered), grad_unnorm, preferred_element_type=jnp.float32
    )
    piece_grad = join_rows(grad_keys_word, grad_keys_ent, grad_values, blocks, words_dev, ents_dev)
    grad_rows = piece_grad
    grad_query_word, grad_query_ent, grad_rows = (grad_query_word, grad_query_ent, grad_rows)
    own_rows = lax.psum_scatter(
        grad_rows.astype(jnp.bfloat16), "seq", scatter_dimension=1, tiled=True
    ).astype(jnp.float32)
    grad_keys = own_rows[..., :model_width]
    grad_values = own_rows[..., model_width:]
    bias_values = jnp.sum(grad_values, axis=(0, 1))
    keys_grad_low = grad_keys.astype(lowered)
    values_grad_low = grad_values.astype(lowered)
    grad_key_w = weight_grad(inputs_low, keys_grad_low)
    grad_value_w = weight_grad(inputs_low, values_grad_low)
    inner_word = grad_query_word.reshape(batch_rows, rows_dev, model_width) * 0.125
    inner_ent = grad_query_ent.reshape(batch_rows, rows_dev, model_width) * 0.125
    bias_query = [
        jnp.sum(inner_word[:, :words_dev], axis=(0, 1)),
        jnp.sum(inner_ent[:, :words_dev], axis=(0, 1)),
        jnp.sum(inner_word[:, words_dev:], axis=(0, 1)),
        jnp.sum(inner_ent[:, words_dev:], axis=(0, 1)),
    ]
    inner_word_low = inner_word.astype(lowered)
    inner_ent_low = inner_ent.astype(lowered)
    grad_query_mats = [
        weight_grad(word_low, inner_word_low[:, :words_dev]),
        weight_grad(word_low, inner_ent_low[:, :words_dev]),
        weight_grad(ent_low, inner_word_low[:, words_dev:]),
        weight_grad(ent_low, inner_ent_low[:, words_dev:]),
    ]
    back_keys = project_back(keys_grad_low, w_attn[4]) + project_back(values_grad_low, w_attn[5])
    back_word = project_back(inner_word_low[:, :words_dev], w_attn[0]) + project_back(
        inner_ent_low[:, :words_dev], w_attn[1]
    )
    back_ent = project_back(inner_word_low[:, words_dev:], w_attn[2]) + project_back(
        inner_ent_low[:, words_dev:], w_attn[3]
    )
    grad_inputs = grad_one + back_keys + jnp.concatenate([back_word, back_ent], 1)
    grad_attn_w = jnp.stack(grad_query_mats + [grad_key_w, grad_value_w, grad_out_proj])
    vec_grad = jnp.concatenate(
        [
            jnp.stack(
                bias_query
                + [bias_values, bias_out, bias_down, gain_one, shift_one, gain_two, shift_two]
            ),
            bias_up.reshape(4, model_width),
        ],
        0,
    )
    rows_attn, rows_up, rows_down = (
        lax.psum_scatter(
            grad_attn_w.astype(jnp.bfloat16), "seq", scatter_dimension=1, tiled=True
        ).astype(jnp.float32),
        lax.psum_scatter(
            grad_up.astype(jnp.bfloat16), "seq", scatter_dimension=0, tiled=True
        ).astype(jnp.float32),
        lax.psum_scatter(
            grad_down.astype(jnp.bfloat16), "seq", scatter_dimension=0, tiled=True
        ).astype(jnp.float32),
    )
    attention_full_gradient = rows_attn + err_attn[0]
    full_up = rows_up + err_up[0]
    full_down = rows_down + err_down[0]
    attention_left_factor = jnp.einsum(
        "vcg,vgo->vco", attention_full_gradient, attention_prior_right, precision=HIGH_PRECISION
    )
    left_up = jnp.dot(full_up, qf_up, precision=HIGH_PRECISION)
    left_down = jnp.dot(full_down, qf_down, precision=HIGH_PRECISION)
    count_attn = attention_full_gradient.shape[1]
    count_up = full_up.shape[0]
    count_down = full_down.shape[0]
    placed_attn = lax.dynamic_update_slice_in_dim(
        jnp.zeros((7, count_attn * seq_count, attention_left_factor.shape[2]), jnp.float32),
        attention_left_factor,
        seq_index * count_attn,
        1,
    )
    placed_up = lax.dynamic_update_slice_in_dim(
        jnp.zeros((count_up * seq_count, left_up.shape[1]), jnp.float32),
        left_up,
        seq_index * count_up,
        0,
    )
    placed_down = lax.dynamic_update_slice_in_dim(
        jnp.zeros((count_down * seq_count, left_down.shape[1]), jnp.float32),
        left_down,
        seq_index * count_down,
        0,
    )
    summed_attn, summed_up, summed_down = lax.psum(
        (placed_attn, placed_up, placed_down), ("seq", "rep")
    )
    orth_attn = jax.vmap(orthonormal)(summed_attn / rep_count)
    orth_up = orthonormal(summed_up / rep_count)
    orth_down = orthonormal(summed_down / rep_count)
    attention_local_gradient = lax.dynamic_slice_in_dim(
        orth_attn, seq_index * count_attn, count_attn, 1
    )
    own_up = lax.dynamic_slice_in_dim(orth_up, seq_index * count_up, count_up, 0)
    own_down = lax.dynamic_slice_in_dim(orth_down, seq_index * count_down, count_down, 0)
    right_parts = (
        jnp.einsum(
            "dpl,dpg->dgl",
            attention_local_gradient,
            attention_full_gradient,
            precision=HIGH_PRECISION,
        ),
        jnp.dot(full_up.T, own_up, precision=HIGH_PRECISION),
        jnp.dot(full_down.T, own_down, precision=HIGH_PRECISION),
        vec_grad,
    )
    attention_right_factor, right_up, right_down, vec_total = lax.psum(
        (right_parts[0], right_parts[1], right_parts[2], right_parts[3]), ("seq", "rep")
    )
    attention_right_factor = attention_right_factor / rep_count
    right_up = right_up / rep_count
    right_down = right_down / rep_count
    vec_mean = vec_total / rep_count
    attention_estimate = jnp.einsum(
        "whg,wng->whn", attention_local_gradient, attention_right_factor, precision=HIGH_PRECISION
    )
    approx_up = jnp.dot(own_up, right_up.T, precision=HIGH_PRECISION)
    approx_down = jnp.dot(own_down, right_down.T, precision=HIGH_PRECISION)
    next_err_attn = (attention_full_gradient - attention_estimate)[None]
    next_err_up = (full_up - approx_up)[None]
    next_err_down = (full_down - approx_down)[None]
    cols_attn = attn_w.shape[2]
    cols_up = up_w.shape[1]
    cols_down = down_w.shape[1]
    step_attn = lax.dynamic_slice_in_dim(attention_estimate, rep_index * cols_attn, cols_attn, 2)
    step_up = lax.dynamic_slice_in_dim(approx_up, rep_index * cols_up, cols_up, 1)
    step_down = lax.dynamic_slice_in_dim(approx_down, rep_index * cols_down, cols_down, 1)
    lr_mat = 1.5 * math.sqrt(rep_count / (SEQS * (WORDS + ENTS)))
    lr_vec = 0.2 * math.sqrt(rep_count / (SEQS * (WORDS + ENTS)))
    next_mom_attn = MOMENTUM * mom_attn + step_attn
    next_mom_up = MOMENTUM * mom_up + step_up
    next_mom_down = MOMENTUM * mom_down + step_down
    next_mom_vecs = MOMENTUM * mom_vecs + vec_mean
    new_attn = attn_w - lr_mat * next_mom_attn
    new_up = up_w - lr_mat * next_mom_up
    new_down = down_w - lr_mat * next_mom_down
    new_vecs = vecs - lr_vec * next_mom_vecs
    return (
        result[:, :words_dev],
        result[:, words_dev:],
        grad_inputs[:, :words_dev],
        grad_inputs[:, words_dev:],
        new_attn,
        new_up,
        new_down,
        new_vecs,
        next_mom_attn,
        next_mom_up,
        next_mom_down,
        next_mom_vecs,
        next_err_attn,
        next_err_up,
        next_err_down,
        attention_local_gradient,
        own_up,
        own_down,
        attention_right_factor,
        right_up,
        right_down,
    )


def solution(mesh):
    in_specs = (
        P("rep", "seq", None),
        P("rep", "seq", None),
        P("rep", "seq", None),
        P("rep", "seq"),
        P("rep", "seq"),
        P("rep", "seq", None),
        P("rep", "seq", None),
        P(None, "seq", "rep"),
        P("seq", "rep"),
        P("seq", "rep"),
        P(),
        P(None, "seq", "rep"),
        P("seq", "rep"),
        P("seq", "rep"),
        P(),
        P("rep", None, "seq", None),
        P("rep", "seq", None),
        P("rep", "seq", None),
        P(),
        P(),
        P(),
    )
    out_specs = (
        P("rep", "seq", None),
        P("rep", "seq", None),
        P("rep", "seq", None),
        P("rep", "seq", None),
        P(None, "seq", "rep"),
        P("seq", "rep"),
        P("seq", "rep"),
        P(),
        P(None, "seq", "rep"),
        P("seq", "rep"),
        P("seq", "rep"),
        P(),
        P("rep", None, "seq", None),
        P("rep", "seq", None),
        P("rep", "seq", None),
        P(None, "seq", None),
        P("seq", None),
        P("seq", None),
        P(),
        P(),
        P(),
    )
    return jax.shard_map(
        on_device, mesh=mesh, in_specs=in_specs, out_specs=out_specs, check_vma=False
    )
```

profile of v0, /device:TPU:0, one launch (start us, length us, event | category | flops | bytes accessed | tf_op | source)
XLA Modules:
  0.0 1053.6 jit_solution(8718621834396332079)
XLA Ops:
  9.6 63.9 %all-gather.8.cloned.1.call-done = bf16[7,192,768]{1,0,2:T(8,128)(2,1)} async-done(((bf16[7,192,96]{1,0,2:T(8,128)(2,1)}), bf16[7,192,768]{1,0,2:T(8,128)(2,1)}) %all-gather.8.cloned.1.call-update) | async-done | bytes 2064400 | tf_op jit(solution)/shard_map/all_gather | solution.py:174
  73.5 4.7 copy.190
  80.7 2.8 fusion.59
  84.6 50.0 %all-gather.10.cloned.1.call-done = bf16[7,768,768]{2,1,0:T(8,128)(2,1)} async-done(((bf16[7,192,768]{2,1,0:T(8,128)(2,1)}), bf16[7,768,768]{2,1,0:T(8,128)(2,1)}) %all-gather.10.cloned.1.call-update) | async-done | bytes 8257552 | tf_op jit(solution)/shard_map/all_gather | solution.py:179
  139.4 38.2 %all-gather.14.cloned.1.call-done = bf16[192,3072]{1,0:T(8,128)(2,1)} async-done(((bf16[192,384]{1,0:T(8,128)(2,1)}), bf16[192,3072]{1,0:T(8,128)(2,1)}) %all-gather.14.cloned.1.call-update) | async-done | bytes 1179664 | tf_op jit(solution)/shard_map/all_gather | solution.py:175
  179.3 5.6 all-reduce
  187.1 33.0 %all-gather.18.cloned.1.call-done = bf16[768,768]{0,1:T(8,128)(2,1)} async-done(((bf16[768,96]{0,1:T(8,128)(2,1)}), bf16[768,768]{0,1:T(8,128)(2,1)}) %all-gather.18.cloned.1.call-update) | async-done | bytes 1179664 | tf_op jit(solution)/shard_map/all_gather | solution.py:176
  224.8 1.9 convolution_add_fusion.10
  230.6 21.0 %all-gather.12.cloned.1.call-done = bf16[1,1152,1536]{2,1,0:T(8,128)(2,1)} async-done(((bf16[1,288,1536]{2,1,0:T(8,128)(2,1)}), bf16[1,1152,1536]{2,1,0:T(8,128)(2,1)}) %all-gather.12.cloned.1.call-update) | async-done | bytes 3538960 | tf_op jit(solution)/shard_map/all_gather | solution.py:210
  251.6 2.1 slice.256
  259.2 2.3 fusion.143
  262.7 2.7 copy.229
  267.1 3.0 fusion.106
  270.1 8.1 fusion.109
  278.2 7.5 fusion.4
  285.7 9.6 exponential_reduce_fusion
  296.1 1.9 copy-done.5
  298.0 4.7 fusion.144
  302.8 2.1 fusion.145
  305.3 12.9 %multiply_convert_fusion = (bf16[288,3072]{1,0:T(8,128)(2,1)}, f32[288,3072]{1,0:T(8,128)}, f32[288,3072]{1,0:T(8,128)}) fusion(f32[3072]{0:T(1024)S(1)} %copy-done.86, bf16[768,3072]{1,0:T(8,128)(2,1)} %all-gather.16.cloned.1.call-done, f32[288,768]{1,0:T(8,128)S(1)} %get-tuple-element.119, f32[768]{0:T(1024)S(1)} %copy-done.90, f32[768]{0:T(1024)S(1)} %copy-done.81, ...), kind=kOutput, calls=%fused_computation.23 | convolution fusion | flops 1418452992 | bytes 14471424 | tf_op jit(solution)/shard_map/thq,qo->tho/dot_general | solution.py:59
  318.2 11.2 %all-gather.20.cloned.1.call-done = bf16[3072,768]{0,1:T(8,128)(2,1)} async-done(((bf16[768,768]{0,1:T(8,128)(2,1)}), bf16[3072,768]{0,1:T(8,128)(2,1)}) %all-gather.20.cloned.1.call-update) | async-done | bytes 4718608 | tf_op jit(solution)/shard_map/all_gather | solution.py:181
  329.5 4.7 fusion.146
  335.5 1.9 fusion.139
  337.5 2.8 fusion.147
  340.3 2.0 multiply_reduce_fusion.2
  342.7 2.6 fusion.50
  345.6 7.7 fusion.5
  353.3 6.0 fusion.18
  360.8 3.8 fusion.15
  367.2 2.4 concatenate.191
  369.6 2.7 copy.201
  373.7 3.9 concatenate.192
  377.6 3.8 copy.202
  382.1 3.1 maximum_maximum_fusion
  386.4 6.4 convolution_convert_fusion
  394.6 5.6 fusion.33
  400.3 2.3 convolution_multiply_fusion
  408.8 17.0 %reduce-scatter.5.cloned.1.call-done = bf16[1,288,1536]{2,1,0:T(8,128)(2,1)} async-done(((bf16[1,1152,1536]{2,1,0:T(8,128)(2,1)}), bf16[1,288,1536]{2,1,0:T(8,128)(2,1)}) %reduce-scatter.5.cloned.1.call-update) | async-done | bytes 884752 | tf_op jit(solution)/shard_map/reduce_scatter | solution.py:293
  425.8 3.0 fusion.28
  428.8 3.0 fusion.30
  433.7 13.4 %copy.210 = bf16[7,768,768]{2,0,1:T(8,128)(2,1)} copy(bf16[7,768,768]{1,2,0:T(8,128)(2,1)} %fusion.32) | data formatting | bytes 16515072 | tf_op jit(solution)/shard_map/stack | solution.py:327
  447.9 6.9 convolution_convert_fusion.1
  456.1 2.1 slice.267
  466.5 1.9 fusion.47
  472.1 2.0 fusion.38
  477.1 3.4 convolution_dynamic-update-slice_fusion
  480.6 76.2 %reduce-scatter.7.cloned.1.call-done = bf16[7,192,768]{2,0,1:T(8,128)(2,1)} async-done(((bf16[7,768,768]{2,0,1:T(8,128)(2,1)}), bf16[7,192,768]{2,0,1:T(8,128)(2,1)}) %reduce-scatter.7.cloned.1.call-update) | async-done | bytes 2064400 | tf_op jit(solution)/shard_map/reduce_scatter | solution.py:339
  556.8 6.6 fusion.58
  564.9 42.5 %reduce-scatter.9.cloned.1.call-done = bf16[192,3072]{1,0:T(8,128)(2,1)} async-done(((bf16[768,3072]{1,0:T(8,128)(2,1)}), bf16[192,3072]{1,0:T(8,128)(2,1)}) %reduce-scatter.9.cloned.1.call-update) | async-done | bytes 1179664 | tf_op jit(solution)/shard_map/reduce_scatter | solution.py:342
  607.3 3.9 fusion.52
  611.6 128.3 %all-reduce.12.cloned.1.call-done = (f32[7,768,8]{1,2,0:T(8,128)}, f32[3072,8]{0,1:T(8,128)}) async-done(((f32[7,768,8]{1,2,0:T(8,128)}, f32[3072,8]{0,1:T(8,128)}), (f32[7,768,8]{1,2,0:T(8,128)}, f32[3072,8]{0,1:T(8,128)})) %all-reduce.12.cloned.1.call-update) | async-done | bytes 270352 | tf_op jit(solution)/shard_map/psum | solution.py:378
  746.7 5.1 custom-call.18
  752.1 4.4 custom-call.19
  757.9 3.4 fusion.53
  761.3 6.2 fusion.57
  767.5 119.5 %all-reduce.8.cloned.1.call-done = (f32[768,8]{0,1:T(8,128)}, f32[768,8]{0,1:T(8,128)}, f32[15,768]{1,0:T(8,128)}) async-done(((f32[768,8]{0,1:T(8,128)}, f32[768,8]{0,1:T(8,128)}, f32[15,768]{1,0:T(8,128)}), (f32[768,8]{0,1:T(8,128)}, f32[768,8]{0,1:T(8,128)}, f32[15,768]{1,0:T(8,128)})) %all-reduce.8.cloned.1.call-update) | async-done | bytes 95248 | tf_op jit(solution)/shard_map/psum | solution.py:378
  887.7 3.5 fusion.150
  891.2 3.3 copy.218
  897.7 4.1 fusion.51
  903.7 4.0 subtract_bitcast_fusion.1
  908.4 121.3 %all-reduce.10.cloned.1.call-done = (f32[7,768,8]{1,2,0:T(8,128)}, f32[3072,8]{0,1:T(8,128)}) async-done(((f32[7,768,8]{1,2,0:T(8,128)}, f32[3072,8]{0,1:T(8,128)}), (f32[7,768,8]{1,2,0:T(8,128)}, f32[3072,8]{0,1:T(8,128)})) %all-reduce.10.cloned.1.call-update) | async-done | bytes 270352 | tf_op jit(solution)/shard_map/psum | solution.py:400
  1030.6 2.0 fusion.149
  1033.7 3.5 fusion.148
  1043.7 2.9 subtract_bitcast_fusion
  (403 shorter events, 92.5 us)
Async XLA Ops:
  7.2 549.6 %copy-start = (f32[7,768,8]{1,2,0:T(8,128)S(1)}, f32[7,768,8]{1,2,0:T(8,128)}, u32[]{:S(2)}) copy-start(f32[7,768,8]{1,2,0:T(8,128)} %param.40) | copy-start | bytes 516100
  7.2 66.3 %all-gather.8.cloned.1.call-start = ((), (), s32[]{:S(2)}) async-start(), calls=%async_computation.4 | async-start | bytes 3538944 | tf_op jit(solution)/shard_map/all_gather | solution.py:174
  9.5 68.8 %copy-start.38 = (f32[192,384]{1,0:T(8,128)S(1)}, f32[192,384]{1,0:T(8,128)}, u32[]{:S(2)}) copy-start(f32[192,384]{1,0:T(8,128)} %param.30) | copy-start | bytes 884740
  9.6 69.5 %copy-start.36 = (f32[768,96]{0,1:T(8,128)S(1)}, f32[768,96]{0,1:T(8,128)}, u32[]{:S(2)}) copy-start(f32[768,96]{0,1:T(8,128)} %param.31) | copy-start | bytes 884740
  9.6 70.3 %copy-start.94 = (s32[1,32,2]{1,2,0:T(2,128)S(1)}, s32[1,32,2]{1,2,0:T(2,128)}, u32[]{:S(2)}) copy-start(s32[1,32,2]{1,2,0:T(2,128)} %param.24) | copy-start | bytes 772
  9.6 70.3 %copy-start.64 = (f32[15,768]{1,0:T(8,128)S(1)}, f32[15,768]{1,0:T(8,128)}, u32[]{:S(2)}) copy-start(f32[15,768]{1,0:T(8,128)} %param.32) | copy-start | bytes 138244
  9.6 125.0 %all-gather.10.cloned.1.call-start = ((), (), s32[]{:S(2)}) async-start(), calls=%async_computation.5 | async-start | bytes 10321920 | tf_op jit(solution)/shard_map/all_gather | solution.py:179
  78.3 99.3 %all-gather.14.cloned.1.call-start = ((), (), s32[]{:S(2)}) async-start(), calls=%async_computation.7 | async-start | bytes 1327104 | tf_op jit(solution)/shard_map/all_gather | solution.py:175
  79.0 141.1 %all-gather.18.cloned.1.call-start = ((), (), s32[]{:S(2)}) async-start(), calls=%async_computation.9 | async-start | bytes 1327104 | tf_op jit(solution)/shard_map/all_gather | solution.py:176
  79.8 171.8 %all-gather.12.cloned.1.call-start = ((), (), s32[]{:S(2)}) async-start(), calls=%async_computation.6 | async-start | bytes 4423680 | tf_op jit(solution)/shard_map/all_gather | solution.py:210
  80.6 105.8 %copy-start.73 = (f32[768]{0:T(1024)}, f32[768]{0:T(1024)S(1)}, u32[]{:S(2)}) copy-start(f32[768]{0:T(1024)S(1)} %get-tuple-element.70) | copy-start | bytes 9220
  84.0 140.8 %copy-start.33 = (bf16[1,32,768]{2,1,0:T(8,128)(2,1)}, bf16[1,32,768]{2,1,0:T(8,128)(2,1)S(1)}, u32[]{:S(2)}) copy-start(bf16[1,32,768]{2,1,0:T(8,128)(2,1)S(1)} %get-tuple-element.107) | copy-start | bytes 147460
  84.6 54.7 %copy-start.50 = (bf16[288,768]{1,0:T(8,128)(2,1)}, bf16[288,768]{1,0:T(8,128)(2,1)S(1)}, u32[]{:S(2)}) copy-start(bf16[288,768]{1,0:T(8,128)(2,1)S(1)} %fusion.62) | copy-start | bytes 1327108
  136.4 41.4 %copy-start.95 = (s32[1,256]{1,0:T(1,128)S(1)}, s32[1,256]{1,0:T(1,128)}, u32[]{:S(2)}) copy-start(s32[1,256]{1,0:T(1,128)} %param.25) | copy-start | bytes 3076
  136.4 41.4 %copy-start.96 = (s32[1,32]{1,0:T(1,128)S(1)}, s32[1,32]{1,0:T(1,128)}, u32[]{:S(2)}) copy-start(s32[1,32]{1,0:T(1,128)} %param.26) | copy-start | bytes 388
  136.4 41.4 %copy-start.97 = (u32[32]{0:T(128)S(1)}, u32[32]{0:T(128)}, u32[]{:S(2)}) copy-start(u32[32]{0:T(128)} %constant.228) | copy-start | bytes 388
  136.4 50.0 %copy-start.7 = (f32[1,256,768]{2,1,0:T(8,128)S(1)}, f32[1,256,768]{2,1,0:T(8,128)}, u32[]{:S(2)}) copy-start(f32[1,256,768]{2,1,0:T(8,128)} %param.27) | copy-start | bytes 2359300
  136.4 50.0 %copy-start.29 = (f32[1,32,768]{2,1,0:T(8,128)S(1)}, f32[1,32,768]{2,1,0:T(8,128)}, u32[]{:S(2)}) copy-start(f32[1,32,768]{2,1,0:T(8,128)} %param.28) | copy-start | bytes 294916
  139.3 166.0 %all-gather.16.cloned.1.call-start = ((), (), s32[]{:S(2)}) async-start(), calls=%async_computation.8 | async-start | bytes 5898240 | tf_op jit(solution)/shard_map/all_gather | solution.py:180
  177.6 151.9 %all-gather.20.cloned.1.call-start = ((), (), s32[]{:S(2)}) async-start(), calls=%async_computation.10 | async-start | bytes 5898240 | tf_op jit(solution)/shard_map/all_gather | solution.py:181
  177.7 49.9 %copy-start.53 = (bf16[1,256,768]{2,1,0:T(8,128)(2,1)}, bf16[1,256,768]{2,1,0:T(8,128)(2,1)S(1)}, u32[]{:S(2)}) copy-start(bf16[1,256,768]{2,1,0:T(8,128)(2,1)S(1)} %slice.204) | copy-start | bytes 1179652
  220.2 205.7 %reduce-scatter.5.cloned.1.call-start = ((), (), s32[]{:S(2)}) async-start(), calls=%async_computation.11 | async-start | bytes 4423680 | tf_op jit(solution)/shard_map/reduce_scatter | solution.py:293
  224.8 45.4 %copy-start.10 = (f32[256,768]{0,1:T(8,128)}, f32[256,768]{0,1:T(8,128)S(1)}, u32[]{:S(2)}) copy-start(f32[256,768]{0,1:T(8,128)S(1)} %copy.191) | copy-start | bytes 2359300
  259.2 11.0 %copy-start.12 = (bf16[1,1024,768]{1,2,0:T(8,128)(2,1)}, bf16[1,1024,768]{1,2,0:T(8,128)(2,1)S(1)}, u32[]{:S(2)}) copy-start(bf16[1,1024,768]{1,2,0:T(8,128)(2,1)S(1)} %copy.227) | copy-start | bytes 4718596
  262.7 15.5 %copy-start.24 = (bf16[1,128,768]{1,2,0:T(8,128)(2,1)}, bf16[1,128,768]{1,2,0:T(8,128)(2,1)S(1)}, u32[]{:S(2)}) copy-start(bf16[1,128,768]{1,2,0:T(8,128)(2,1)S(1)} %copy.228) | copy-start | bytes 589828
  278.2 17.9 %slice-start = ((s8[14155776]{0:T(1024)(128)(4,1)}), s8[4194304]{0:T(1024)(128)(4,1)S(1)}, s32[]{:S(2)}) async-start(s8[14155776]{0:T(1024)(128)(4,1)} %bitcast.318), calls=%async_computation.18 | async-start | bytes 8388608
  278.2 17.9 %slice-start.1 = ((s8[14155776]{0:T(1024)(128)(4,1)}), s8[1572864]{0:T(1024)(128)(4,1)S(1)}, s32[]{:S(2)}) async-start(s8[14155776]{0:T(1024)(128)(4,1)} %bitcast.318), calls=%async_computation.19 | async-start | bytes 3145728
  285.7 10.2 copy-start.57
  285.7 10.2 copy-start.15
  285.7 10.2 copy-start.43
  285.7 10.5 slice-start.2
  285.7 10.5 slice-start.3
  295.9 6.8 copy-start.79
  305.0 37.3 %copy-start.17 = (f32[288,768]{1,0:T(8,128)}, f32[288,768]{1,0:T(8,128)S(1)}, u32[]{:S(2)}) copy-start(f32[288,768]{1,0:T(8,128)S(1)} %get-tuple-element.119) | copy-start | bytes 2654212
  305.3 37.0 %copy-start.88 = (f32[288]{0:T(512)}, f32[288]{0:T(512)S(1)}, u32[]{:S(2)}) copy-start(f32[288]{0:T(512)S(1)} %add_rsqrt_fusion.1) | copy-start | bytes 3460
  305.3 24.2 %copy-start.92 = (f32[768]{0:T(1024)S(1)}, f32[768]{0:T(1024)}, u32[]{:S(2)}) copy-start(f32[768]{0:T(1024)} %get-tuple-element.71) | copy-start | bytes 9220
  329.5 7.9 slice-start.11
  329.5 7.9 slice-start.12
  329.5 7.9 copy-start.100
  337.4 8.1 slice-start.4
  337.4 8.1 slice-start.5
  337.4 8.1 slice-start.6
  345.6 7.7 copy-start.11
  372.7 8.7 slice-start.8
  385.2 91.9 %reduce-scatter.11.cloned.1.call-start = ((), (), s32[]{:S(2)}) async-start(), calls=%async_computation.14 | async-start | bytes 5898240 | tf_op jit(solution)/shard_map/reduce_scatter | solution.py:345
  392.8 7.5 copy-start.25
  392.8 164.0 %reduce-scatter.7.cloned.1.call-start = ((), (), s32[]{:S(2)}) async-start(), calls=%async_computation.12 | async-start | bytes 11796480 | tf_op jit(solution)/shard_map/reduce_scatter | solution.py:339
  407.3 24.5 %copy-start.48 = (bf16[1,288,12,64]{1,3,2,0:T(8,128)(2,1)S(1)}, bf16[1,288,12,64]{1,3,2,0:T(8,128)(2,1)}, u32[]{:S(2)}) copy-start(bf16[1,288,12,64]{1,3,2,0:T(8,128)(2,1)} %copy-done.47) | copy-start | bytes 1327108
  447.2 160.2 %reduce-scatter.9.cloned.1.call-start = ((), (), s32[]{:S(2)}) async-start(), calls=%async_computation.13 | async-start | bytes 5898240 | tf_op jit(solution)/shard_map/reduce_scatter | solution.py:342
  454.8 7.9 copy-start.85
  454.9 7.9 copy-start.83
  454.9 285.0 %all-reduce.12.cloned.1.call-start = ((), (), s32[]{:S(2)}) async-start(), calls=%async_computation.17 | async-start | bytes 540672 | tf_op jit(solution)/shard_map/psum | solution.py:378
  456.0 8.6 copy-start.19
  480.6 83.3 %copy-start.52 = (f32[3072,8]{0,1:T(8,128)}, f32[3072,8]{0,1:T(8,128)S(1)}, u32[]{:S(2)}) copy-start(f32[3072,8]{0,1:T(8,128)S(1)} %convolution_dynamic-update-slice_fusion) | copy-start | bytes 294916
  480.6 126.8 %copy-start.69 = (f32[3072,8]{0,1:T(8,128)S(1)}, f32[3072,8]{0,1:T(8,128)}, u32[]{:S(2)}) copy-start(f32[3072,8]{0,1:T(8,128)} %param.41) | copy-start | bytes 294916
  564.6 322.4 %all-reduce.8.cloned.1.call-start = ((), (), s32[]{:S(2)}) async-start(), calls=%async_computation.15 | async-start | bytes 196608 | tf_op jit(solution)/shard_map/psum | solution.py:378
  611.6 149.7 %copy-start.67 = (f32[768,8]{0,1:T(8,128)}, f32[768,8]{0,1:T(8,128)S(1)}, u32[]{:S(2)}) copy-start(f32[768,8]{0,1:T(8,128)S(1)} %dynamic_update_slice.10) | copy-start | bytes 73732
  745.1 142.6 %copy-start.61 = (f32[768,8]{0,1:T(8,128)}, f32[768,8]{0,1:T(8,128)S(1)}, u32[]{:S(2)}) copy-start(f32[768,8]{0,1:T(8,128)S(1)} %constant_dynamic-slice_fusion) | copy-start | bytes 73732
  757.8 275.8 %copy-start.49 = (f32[7,192,8]{1,2,0:T(8,128)}, f32[7,192,8]{1,2,0:T(8,128)S(1)}, u32[]{:S(2)}) copy-start(f32[7,192,8]{1,2,0:T(8,128)S(1)} %constant_dynamic-slice_fusion.2) | copy-start | bytes 129028
  761.3 268.5 %all-reduce.10.cloned.1.call-start = ((), (), s32[]{:S(2)}) async-start(), calls=%async_computation.16 | async-start | bytes 540672 | tf_op jit(solution)/shard_map/psum | solution.py:400
  887.7 6.8 copy-start.78
  891.2 10.7 %copy-start.37 = (f32[768,96]{0,1:T(8,128)S(1)}, f32[768,96]{0,1:T(8,128)}, u32[]{:S(2)}) copy-start(f32[768,96]{0,1:T(8,128)} %param.31) | copy-start | bytes 884740
  891.2 10.7 %copy-start.59 = (f32[768,96]{0,1:T(8,128)S(1)}, f32[768,96]{0,1:T(8,128)}, u32[]{:S(2)}) copy-start(f32[768,96]{0,1:T(8,128)} %param.35) | copy-start | bytes 884740
  897.7 132.9 %copy-start.72 = (f32[192,8]{0,1:T(8,128)}, f32[192,8]{0,1:T(8,128)S(1)}, u32[]{:S(2)}) copy-start(f32[192,8]{0,1:T(8,128)S(1)} %constant_dynamic-slice_fusion.1) | copy-start | bytes 18436
  (64 other events, 234.6 us)
Sparse Core Ops, SparseCore 0:
  10.8 62.7 all-gather.7
  78.4 56.1 all-gather.9
  137.2 40.3 all-gather.13
  180.2 39.8 all-gather.17
  222.1 29.4 all-gather.11
  253.0 37.4 all-gather.15
  292.0 37.4 all-gather.19
  385.4 40.3 reduce-scatter.4
  428.4 47.9 reduce-scatter.10
  478.8 77.9 reduce-scatter.6
  559.3 47.9 reduce-scatter.8
  613.2 126.6 all-reduce.11
  761.4 125.5 all-reduce.7
  902.0 127.6 all-reduce.9
where the time goes:
time: 1060 us; the launch traced here: 1050 us
  waiting for transfers between devices  722 us (68%)
  matrix products  161 us (15%)
  local copies, waits for them, and re-layouts  79.4 us (7%)
  other arithmetic  66.9 us (6%)
  between operations  16.9 us (2%)
    psum x2, waiting for transfers between devices, on_device(): lax.psum((placed_attn, placed_up, placed_down), ('seq', 'rep'))  248 us
    psum x1, waiting for transfers between devices, on_device(): lax.psum((right_parts[0], right_parts[1], right_parts[2], right_parts[3])...  121 us
    reduce_scatter x1, waiting for transfers between devices, on_device(): lax.psum_scatter(grad_attn_w.astype(jnp.bfloat16), 'seq', scatter_dimensi...  76.2 us
    all_gather x1, waiting for transfers between devices, on_device(): lax.all_gather(attn_w.astype(lowered), 'rep', axis=2, tiled=True)  63.9 us
    all_gather x1, waiting for transfers between devices, on_device(): lax.all_gather(column_parts[0], 'seq', axis=1, tiled=True)  50 us
    reduce_scatter x1, waiting for transfers between devices, on_device(): lax.psum_scatter(grad_up.astype(jnp.bfloat16), 'seq', scatter_dimension=0...  42.5 us
    all_gather x1, waiting for transfers between devices, on_device(): lax.all_gather(up_w.astype(lowered), 'rep', axis=1, tiled=True)  38.2 us
    all_gather x1, waiting for transfers between devices, on_device(): lax.all_gather(down_w.astype(lowered), 'rep', axis=1, tiled=True)  33 us
  transfers between devices with their start and end apart: 14, of which 12 were waited for; matrix products, arithmetic and copies ran while one was open for 17% of the time, Pallas kernels for 0%

commit v1 on v0

--- a/solution.py
+++ b/solution.py
@@ -1,8 +1,11 @@
+import functools
 import math
 
 import jax
 import jax.numpy as jnp
 from jax import lax
+from jax.experimental import pallas as pl
+from jax.experimental.pallas import tpu as pltpu
 from jax.sharding import PartitionSpec as P
 
 HEADS = 12
@@ -453,6 +456,523 @@
     )
 
 
+def seq_swap(array, bits):
+    size = lax.axis_size("seq")
+    return lax.ppermute(array, "seq", [(i, i ^ bits) for i in range(size)])
+
+
+def rep_swap(array, bits):
+    size = lax.axis_size("rep")
+    return lax.ppermute(array, "rep", [(i, i ^ bits) for i in range(size)])
+
+
+def planes_swap(array):
+    seqs, reps = lax.axis_size("seq"), lax.axis_size("rep")
+    pairs = []
+    for s in range(seqs):
+        for r in range(reps):
+            pairs.append((s * reps + r, (r // 2) * reps + 2 * s + r % 2))
+    return lax.ppermute(array, ("seq", "rep"), pairs)
+
+
+def gather_seq(piece):
+    other_chip = seq_swap(piece, 2)
+    other_core = seq_swap(piece, 1)
+    return [piece, other_core, other_chip, seq_swap(other_chip, 1)]
+
+
+def ordered(bit, mine, other, axis):
+    return jnp.where(
+        bit == 0, jnp.stack([mine, other], axis), jnp.stack([other, mine], axis)
+    )
+
+
+def gather_rep(piece):
+    rep_index = lax.axis_index("rep")
+    side, level, far = rep_index % 2, (rep_index // 2) % 2, rep_index // 4
+    pair = ordered(far, piece, rep_swap(piece, 4), 0)
+    pair_side = rep_swap(pair, 1)
+    next_pair = rep_swap(pair, 2)
+    next_side = rep_swap(next_pair, 1)
+    mine = ordered(level, pair, next_pair, 1)
+    other = ordered(level, pair_side, next_side, 1)
+    return ordered(side, mine, other, 2).reshape((4, 2) + piece.shape)
+
+
+def join_pieces(pieces, words_dev):
+    return jnp.concatenate(
+        [piece[:words_dev] for piece in pieces] + [piece[words_dev:] for piece in pieces], 0
+    )
+
+
+def scatter_rows(full, words_dev, ents_dev):
+    count = 4
+    first_ent = count * words_dev
+
+    def rows(k):
+        return [
+            full[k * words_dev : (k + 1) * words_dev],
+            full[first_ent + k * ents_dev : first_ent + (k + 1) * ents_dev],
+        ]
+
+    rows_dev = words_dev + ents_dev
+    got = seq_swap(jnp.concatenate(rows(1) + rows(3), 0).astype(jnp.bfloat16), 1)
+    got = got.astype(jnp.float32)
+    mine = jnp.concatenate(rows(0), 0) + got[:rows_dev]
+    other = jnp.concatenate(rows(2), 0) + got[rows_dev:]
+    return mine + seq_swap(other.astype(jnp.bfloat16), 2).astype(jnp.float32)
+
+
+def rows_norm(hidden, gain, shift):
+    center = hidden - jnp.mean(hidden, -1, keepdims=True)
+    rstd = lax.rsqrt(jnp.mean(center * center, -1, keepdims=True) + EPS)
+    normed = center * rstd
+    return (normed * gain + shift, normed, rstd)
+
+
+def rows_norm_back(grad, normed, rstd, gain):
+    dnormed = grad * gain
+    grad_in = rstd * (
+        dnormed
+        - jnp.mean(dnormed, -1, keepdims=True)
+        - normed * jnp.mean(dnormed * normed, -1, keepdims=True)
+    )
+    return (grad_in, jnp.sum(grad * normed, axis=0), jnp.sum(grad, axis=0))
+
+
+def mm(left, right, left_dim=1, right_dim=0):
+    return lax.dot_general(
+        left, right, (((left_dim,), (right_dim,)), ((), ())), preferred_element_type=jnp.float32
+    )
+
+
+def nt_dot(left, right):
+    return mm(left, right, 1, 1)
+
+
+def tn_dot(left, right):
+    return mm(left, right, 0, 0)
+
+
+HEAD_DIM = 64
+
+
+def attention_kernel(word_count, heads, query_ref, key_ref, offset_ref, attn_ref, low_ref, stat_ref):
+    width = heads * HEAD_DIM
+    rows = query_ref.shape[0]
+    lane = lax.broadcasted_iota(jnp.int32, (rows, 128), 1)
+    stats = jnp.zeros((rows, 128), jnp.float32)
+    for h in range(heads):
+        low, high = h * HEAD_DIM, (h + 1) * HEAD_DIM
+        q_word = query_ref[:, low:high]
+        q_ent = query_ref[:, width + low : width + high]
+        k_word = key_ref[:word_count, 2 * width + low : 2 * width + high]
+        k_ent = key_ref[word_count:, 2 * width + low : 2 * width + high]
+        s_word = nt_dot(q_word, k_word) + offset_ref[:, :word_count]
+        s_ent = nt_dot(q_ent, k_ent) + offset_ref[:, word_count:]
+        top = jnp.maximum(
+            jnp.max(s_word, -1, keepdims=True), jnp.max(s_ent, -1, keepdims=True)
+        )
+        w_word = jnp.exp(s_word - top)
+        w_ent = jnp.exp(s_ent - top)
+        total = jnp.sum(w_word, -1, keepdims=True) + jnp.sum(w_ent, -1, keepdims=True)
+        v_word = key_ref[:word_count, 3 * width + low : 3 * width + high]
+        v_ent = key_ref[word_count:, 3 * width + low : 3 * width + high]
+        unnorm = mm(w_word.astype(jnp.bfloat16), v_word) + mm(w_ent.astype(jnp.bfloat16), v_ent)
+        attn = unnorm / total
+        attn_ref[:, low:high] = attn
+        low_ref[:, low:high] = attn.astype(jnp.bfloat16)
+        stats = jnp.where(lane == h, top, stats)
+        stats = jnp.where(lane == heads + h, total, stats)
+    stat_ref[...] = stats
+
+
+def attention_forward(packed, offsets, word_count, heads, block):
+    count, packed_width = packed.shape
+    width = heads * HEAD_DIM
+    return pl.pallas_call(
+        functools.partial(attention_kernel, word_count, heads),
+        grid=(count // block,),
+        in_specs=[
+            pl.BlockSpec((block, packed_width), lambda i: (i, 0)),
+            pl.BlockSpec((count, packed_width), lambda i: (0, 0)),
+            pl.BlockSpec((1, count), lambda i: (0, 0)),
+        ],
+        out_specs=[
+            pl.BlockSpec((block, width), lambda i: (i, 0)),
+            pl.BlockSpec((block, width), lambda i: (i, 0)),
+            pl.BlockSpec((block, 128), lambda i: (i, 0)),
+        ],
+        out_shape=[
+            jax.ShapeDtypeStruct((count, width), jnp.float32),
+            jax.ShapeDtypeStruct((count, width), jnp.bfloat16),
+            jax.ShapeDtypeStruct((count, 128), jnp.float32),
+        ],
+        compiler_params=pltpu.CompilerParams(dimension_semantics=("arbitrary",)),
+        cost_estimate=pl.CostEstimate(
+            flops=4 * count * count * width,
+            bytes_accessed=6 * count * packed_width,
+            transcendentals=count * count * heads,
+        ),
+        name="attention",
+    )(packed, packed, offsets)
+
+
+def attention_back_kernel(
+    word_count,
+    heads,
+    query_ref,
+    key_ref,
+    offset_ref,
+    attn_ref,
+    stat_ref,
+    grad_ref,
+    dquery_ref,
+    dkey_ref,
+    dvalue_ref,
+    key_sum,
+    value_sum,
+):
+    width = heads * HEAD_DIM
+    step = pl.program_id(0)
+
+    @pl.when(step == 0)
+    def _():
+        key_sum[...] = jnp.zeros_like(key_sum)
+        value_sum[...] = jnp.zeros_like(value_sum)
+
+    for h in range(heads):
+        low, high = h * HEAD_DIM, (h + 1) * HEAD_DIM
+        q_word = query_ref[:, low:high]
+        q_ent = query_ref[:, width + low : width + high]
+        k_word = key_ref[:word_count, 2 * width + low : 2 * width + high]
+        k_ent = key_ref[word_count:, 2 * width + low : 2 * width + high]
+        v_word = key_ref[:word_count, 3 * width + low : 3 * width + high]
+        v_ent = key_ref[word_count:, 3 * width + low : 3 * width + high]
+        top = stat_ref[:, h : h + 1]
+        inverse = 1.0 / stat_ref[:, heads + h : heads + h + 1]
+        grad = grad_ref[:, low:high]
+        delta = jnp.sum(grad * attn_ref[:, low:high], -1, keepdims=True) * inverse
+        grad_low = (grad * inverse).astype(jnp.bfloat16)
+        w_word = jnp.exp(nt_dot(q_word, k_word) + offset_ref[:, :word_count] - top)
+        w_ent = jnp.exp(nt_dot(q_ent, k_ent) + offset_ref[:, word_count:] - top)
+        d_word = (w_word * (nt_dot(grad_low, v_word) - delta)).astype(jnp.bfloat16)
+        d_ent = (w_ent * (nt_dot(grad_low, v_ent) - delta)).astype(jnp.bfloat16)
+        dquery_ref[:, low:high] = mm(d_word, k_word)
+        dquery_ref[:, width + low : width + high] = mm(d_ent, k_ent)
+        key_sum[low:high, :word_count] += tn_dot(q_word, d_word)
+        key_sum[low:high, word_count:] += tn_dot(q_ent, d_ent)
+        value_sum[low:high, :word_count] += tn_dot(grad_low, w_word.astype(jnp.bfloat16))
+        value_sum[low:high, word_count:] += tn_dot(grad_low, w_ent.astype(jnp.bfloat16))
+
+    @pl.when(step == pl.num_programs(0) - 1)
+    def _():
+        dkey_ref[...] = key_sum[...].T
+        dvalue_ref[...] = value_sum[...].T
+
+
+def attention_backward(packed, offsets, attn, stats, grad, word_count, heads, block):
+    count, packed_width = packed.shape
+    width = heads * HEAD_DIM
+    return pl.pallas_call(
+        functools.partial(attention_back_kernel, word_count, heads),
+        grid=(count // block,),
+        in_specs=[
+            pl.BlockSpec((block, packed_width), lambda i: (i, 0)),
+            pl.BlockSpec((count, packed_width), lambda i: (0, 0)),
+            pl.BlockSpec((1, count), lambda i: (0, 0)),
+            pl.BlockSpec((block, width), lambda i: (i, 0)),
+            pl.BlockSpec((block, 128), lambda i: (i, 0)),
+            pl.BlockSpec((block, width), lambda i: (i, 0)),
+        ],
+        out_specs=[
+            pl.BlockSpec((block, 2 * width), lambda i: (i, 0)),
+            pl.BlockSpec((count, width), lambda i: (0, 0)),
+            pl.BlockSpec((count, width), lambda i: (0, 0)),
+        ],
+        out_shape=[
+            jax.ShapeDtypeStruct((count, 2 * width), jnp.float32),
+            jax.ShapeDtypeStruct((count, width), jnp.float32),
+            jax.ShapeDtypeStruct((count, width), jnp.float32),
+        ],
+        scratch_shapes=[
+            pltpu.VMEM((width, count), jnp.float32),
+            pltpu.VMEM((width, count), jnp.float32),
+        ],
+        compiler_params=pltpu.CompilerParams(dimension_semantics=("arbitrary",)),
+        cost_estimate=pl.CostEstimate(
+            flops=10 * count * count * width,
+            bytes_accessed=16 * count * packed_width,
+            transcendentals=count * count * heads,
+        ),
+        name="attention_back",
+    )(packed, packed, offsets, attn, stats, grad)
+
+
+def tall(left):
+    return jnp.swapaxes(left, -1, -2)
+
+
+def head_split_device(
+    x_words,
+    x_ents,
+    spans,
+    word_mask,
+    ent_mask,
+    cot_words,
+    cot_ents,
+    attn_w,
+    up_w,
+    down_w,
+    vecs,
+    mom_attn,
+    mom_up,
+    mom_down,
+    mom_vecs,
+    err_attn,
+    err_up,
+    err_down,
+    attention_prior_right,
+    qf_up,
+    qf_down,
+):
+    low_type = jnp.bfloat16
+    words_dev, width = x_words.shape[1:]
+    ents_dev = x_ents.shape[1]
+    rows_dev = words_dev + ents_dev
+    seq_count, rep_count = lax.axis_size("seq"), lax.axis_size("rep")
+    seq_index, rep_index = lax.axis_index("seq"), lax.axis_index("rep")
+    heads = HEADS // seq_count
+    part = width // seq_count
+    word_count = words_dev * seq_count
+    ent_count = ents_dev * seq_count
+    cols = attn_w.shape[2]
+    cols_up = up_w.shape[1]
+    hidden = cols_up * rep_count
+    hidden_part = hidden // seq_count
+
+    project_piece = jnp.swapaxes(attn_w[:6].astype(low_type), 0, 1).reshape(part, 6 * cols)
+    project_all = gather_rep(planes_swap(project_piece))
+    out_all = gather_rep(attn_w[6].astype(low_type).T)
+    up_all = gather_rep(planes_swap(up_w.astype(low_type)))
+    down_all = gather_rep(down_w.astype(low_type).T)
+    w_project = jnp.transpose(
+        project_all.reshape(4, 2, part, 6, cols), (0, 2, 3, 1, 4)
+    ).reshape(width, 6, part)
+    w_out = out_all.reshape(width, part)
+    w_up = jnp.transpose(up_all, (0, 2, 1, 3)).reshape(width, hidden_part)
+    w_down = down_all.reshape(width, hidden_part)
+
+    inputs = jnp.concatenate([x_words[0], x_ents[0] + span_mean(spans[0], width)], 0)
+    live = jnp.concatenate([word_mask[0], ent_mask[0]], 0).astype(low_type)
+    live = jnp.pad(live, (0, 16 * width - rows_dev)).reshape(16, width)
+    pieces = gather_seq(jnp.concatenate([inputs.astype(low_type), live], 0))
+    rows_low = join_pieces([piece[:rows_dev] for piece in pieces], words_dev)
+    lives = [piece[rows_dev:].reshape(-1)[:rows_dev] for piece in pieces]
+    offsets = (join_pieces(lives, words_dev).astype(jnp.float32) - 1.0) * MASK_FILL
+    offsets = offsets.reshape(1, -1)
+
+    own_vecs = lax.dynamic_slice_in_dim(vecs, seq_index * part, part, 1)
+    none = jnp.zeros((part,), jnp.float32)
+    scale = jnp.where(jnp.arange(4 * part) < 2 * part, 0.125, 1.0).astype(jnp.float32)
+    w_word = jnp.concatenate([w_project[:, j] for j in (0, 1, 4, 5)], -1)
+    w_ent = jnp.concatenate([w_project[:, j] for j in (2, 3, 4, 5)], -1)
+    bias_word = jnp.concatenate([own_vecs[0], own_vecs[1], none, own_vecs[4]])
+    bias_ent = jnp.concatenate([own_vecs[2], own_vecs[3], none, own_vecs[4]])
+    packed = jnp.concatenate(
+        [
+            ((mm(rows_low[:word_count], w_word) + bias_word) * scale).astype(low_type),
+            ((mm(rows_low[word_count:], w_ent) + bias_ent) * scale).astype(low_type),
+        ],
+        0,
+    )
+    attn, attn_low, stats = attention_forward(packed, offsets, word_count, heads, rows_dev)
+
+    branch = scatter_rows(nt_dot(attn_low, w_out), words_dev, ents_dev) + vecs[5]
+    mid, normed_one, rstd_one = rows_norm(inputs + branch, vecs[7], vecs[8])
+    mid_low = join_pieces(gather_seq(mid.astype(low_type)), words_dev)
+    bias_up = lax.dynamic_slice_in_dim(
+        vecs[11:15].reshape(hidden), seq_index * hidden_part, hidden_part, 0
+    )
+    pre = mm(mid_low, w_up) + bias_up
+    act_low = gelu_exact(pre).astype(low_type)
+    ffn = scatter_rows(nt_dot(act_low, w_down), words_dev, ents_dev) + vecs[6]
+    result, normed_two, rstd_two = rows_norm(mid + ffn, vecs[9], vecs[10])
+
+    grad_result = jnp.concatenate([cot_words[0], cot_ents[0]], 0)
+    grad_two, gain_two, shift_two = rows_norm_back(grad_result, normed_two, rstd_two, vecs[9])
+    bias_down = jnp.sum(grad_two, 0)
+    grad_ffn = join_pieces(gather_seq(grad_two.astype(low_type)), words_dev)
+    grad_act = mm(grad_ffn, w_down)
+    unused_value, gelu_pull = jax.vjp(gelu_exact, pre)
+    grad_pre = gelu_pull(grad_act)[0]
+    grad_bias_up = jnp.sum(grad_pre, 0)
+    grad_pre_low = grad_pre.astype(low_type)
+    grad_mid = grad_two + scatter_rows(nt_dot(grad_pre_low, w_up), words_dev, ents_dev)
+    grad_down = tn_dot(act_low, grad_ffn)
+    grad_up = tn_dot(mid_low, grad_pre_low).astype(low_type)
+    grad_up = lax.all_to_all(grad_up.reshape(seq_count, part, hidden_part), "seq", 0, 0)
+    grad_up = jnp.swapaxes(grad_up, 0, 1).reshape(part, hidden).astype(jnp.float32)
+
+    grad_one, gain_one, shift_one = rows_norm_back(grad_mid, normed_one, rstd_one, vecs[7])
+    bias_out = jnp.sum(grad_one, 0)
+    grad_branch = join_pieces(gather_seq(grad_one.astype(low_type)), words_dev)
+    grad_out = tn_dot(attn_low, grad_branch)
+    grad_attn = mm(grad_branch, w_out)
+    dquery, dkey, dvalue = attention_backward(
+        packed, offsets, attn, stats, grad_attn, word_count, heads, rows_dev
+    )
+    dquery = dquery * 0.125
+    dkey_low = dkey.astype(low_type)
+    dvalue_low = dvalue.astype(low_type)
+    dquery_low = dquery.astype(low_type)
+    d_low = jnp.concatenate([dquery_low, dkey_low, dvalue_low], 1)
+    grad_inputs = grad_one + scatter_rows(
+        jnp.concatenate(
+            [nt_dot(d_low[:word_count], w_word), nt_dot(d_low[word_count:], w_ent)], 0
+        ),
+        words_dev,
+        ents_dev,
+    )
+    rows_word, rows_ent = rows_low[:word_count], rows_low[word_count:]
+    grad_project = jnp.concatenate(
+        [
+            tn_dot(rows_word, dquery_low[:word_count]),
+            tn_dot(rows_ent, dquery_low[word_count:]),
+            tn_dot(rows_low, jnp.concatenate([dkey_low, dvalue_low], 1)),
+        ],
+        1,
+    ).astype(low_type)
+    grad_project = lax.all_to_all(
+        grad_project.reshape(seq_count, part, 6 * part), "seq", 0, 0
+    )
+    grad_project = jnp.transpose(
+        grad_project.reshape(seq_count, part, 6, part), (2, 1, 0, 3)
+    ).reshape(6, part, width)
+
+    bias_query = jnp.stack(
+        [
+            jnp.sum(dquery[:word_count, :part], 0),
+            jnp.sum(dquery[:word_count, part:], 0),
+            jnp.sum(dquery[word_count:, :part], 0),
+            jnp.sum(dquery[word_count:, part:], 0),
+            jnp.sum(dvalue, 0),
+        ]
+    )
+    vec_grad = jnp.zeros((15, width), jnp.float32)
+    vec_grad = lax.dynamic_update_slice(vec_grad, bias_query, (0, seq_index * part))
+    vec_grad = lax.dynamic_update_slice(
+        vec_grad,
+        jnp.stack([bias_out, bias_down, gain_one, shift_one, gain_two, shift_two]),
+        (5, 0),
+    )
+    bias_rows = hidden_part // width
+    vec_grad = lax.dynamic_update_slice(
+        vec_grad, grad_bias_up.reshape(bias_rows, width), (11 + seq_index * bias_rows, 0)
+    )
+
+    full_attn = jnp.concatenate([grad_project.astype(jnp.float32), grad_out[None]], 0) + err_attn[0]
+    full_up = grad_up + err_up[0]
+    full_down = grad_down + err_down[0]
+    left_attn = jnp.einsum(
+        "jcg,jgr->jrc", full_attn, attention_prior_right, precision=HIGH_PRECISION
+    )
+    left_up = jnp.einsum("cg,gr->rc", full_up, qf_up, precision=HIGH_PRECISION)
+    left_down = jnp.einsum("cg,gr->rc", full_down, qf_down, precision=HIGH_PRECISION)
+    rank = qf_up.shape[1]
+    left = jnp.concatenate(
+        [jnp.swapaxes(left_attn, 0, 1).reshape(rank, 7 * part), left_up, left_down], 1
+    )
+    for bits in (1, 2, 4):
+        left = left + rep_swap(left, bits)
+    left = left / rep_count
+    left_attn = jnp.swapaxes(left[:, : 7 * part].reshape(rank, 7, part), 0, 1)
+    left_up = left[:, 7 * part : 8 * part]
+    left_down = left[:, 8 * part :]
+    gram = jnp.concatenate(
+        [
+            jnp.einsum("jrc,jtc->jrt", left_attn, left_attn, precision=HIGH_PRECISION),
+            jnp.einsum("rc,tc->rt", left_up, left_up, precision=HIGH_PRECISION)[None],
+            jnp.einsum("rc,tc->rt", left_down, left_down, precision=HIGH_PRECISION)[None],
+        ],
+        0,
+    )
+    gram = gram + seq_swap(gram, 1)
+    gram = gram + seq_swap(gram, 2)
+    lower = jnp.linalg.cholesky(gram)
+    inverse = jax.scipy.linalg.solve_triangular(
+        lower, jnp.broadcast_to(jnp.eye(rank, dtype=jnp.float32), lower.shape), lower=True
+    )
+    orth_attn = jnp.einsum("jrt,jtc->jrc", inverse[:7], left_attn, precision=HIGH_PRECISION)
+    orth_up = jnp.dot(inverse[7], left_up, precision=HIGH_PRECISION)
+    orth_down = jnp.dot(inverse[8], left_down, precision=HIGH_PRECISION)
+    right = jnp.concatenate(
+        [
+            jnp.swapaxes(
+                jnp.einsum("jrc,jcg->jrg", orth_attn, full_attn, precision=HIGH_PRECISION), 0, 1
+            ).reshape(rank, 7 * width),
+            jnp.dot(orth_up, full_up, precision=HIGH_PRECISION),
+            jnp.dot(orth_down, full_down, precision=HIGH_PRECISION),
+            vec_grad.reshape(rank, -1),
+        ],
+        1,
+    )
+    right_size = right.shape[1]
+    right = jnp.pad(right, ((0, 0), (0, -right_size % 512)))
+    core, chip = seq_index % 2, seq_index // 2
+    for bits, bit in ((1, core), (2, chip)):
+        half = right.shape[1] // 2
+        below, above = right[:, :half], right[:, half:]
+        right = jnp.where(bit == 0, below, above) + seq_swap(
+            jnp.where(bit == 0, above, below), bits
+        )
+    for bits in (1, 2, 4):
+        right = right + rep_swap(right, bits)
+    for bits, bit in ((2, chip), (1, core)):
+        right = ordered(bit, right, seq_swap(right, bits), 1).reshape(rank, -1)
+    right = right / rep_count
+    right_attn = jnp.swapaxes(right[:, : 7 * width].reshape(rank, 7, width), 0, 1)
+    right_up = right[:, 7 * width : 7 * width + hidden]
+    right_down = right[:, 7 * width + hidden : 8 * width + hidden]
+    vec_mean = right[:, 8 * width + hidden : right_size].reshape(15, width)
+
+    approx_attn = jnp.einsum("jrc,jrg->jcg", orth_attn, right_attn, precision=HIGH_PRECISION)
+    approx_up = jnp.einsum("rc,rg->cg", orth_up, right_up, precision=HIGH_PRECISION)
+    approx_down = jnp.einsum("rc,rg->cg", orth_down, right_down, precision=HIGH_PRECISION)
+    step_attn = lax.dynamic_slice_in_dim(approx_attn, rep_index * cols, cols, 2)
+    step_up = lax.dynamic_slice_in_dim(approx_up, rep_index * cols_up, cols_up, 1)
+    step_down = lax.dynamic_slice_in_dim(approx_down, rep_index * cols, cols, 1)
+    lr_mat = 1.5 * math.sqrt(rep_count / (SEQS * (WORDS + ENTS)))
+    lr_vec = 0.2 * math.sqrt(rep_count / (SEQS * (WORDS + ENTS)))
+    next_mom_attn = MOMENTUM * mom_attn + step_attn
+    next_mom_up = MOMENTUM * mom_up + step_up
+    next_mom_down = MOMENTUM * mom_down + step_down
+    next_mom_vecs = MOMENTUM * mom_vecs + vec_mean
+    return (
+        result[None, :words_dev],
+        result[None, words_dev:],
+        grad_inputs[None, :words_dev],
+        grad_inputs[None, words_dev:],
+        attn_w - lr_mat * next_mom_attn,
+        up_w - lr_mat * next_mom_up,
+        down_w - lr_mat * next_mom_down,
+        vecs - lr_vec * next_mom_vecs,
+        next_mom_attn,
+        next_mom_up,
+        next_mom_down,
+        next_mom_vecs,
+        (full_attn - approx_attn)[None],
+        (full_up - approx_up)[None],
+        (full_down - approx_down)[None],
+        tall(orth_attn),
+        tall(orth_up),
+        tall(orth_down),
+        tall(right_attn),
+        tall(right_up),
+        tall(right_down),
+    )
+
+
 def solution(mesh):
     in_specs = (
         P("rep", "seq", None),
@@ -500,6 +1020,9 @@
         P(),
         P(),
     )
+    seqs, reps = mesh.shape["seq"], mesh.shape["rep"]
+    split_heads = seqs == 4 and reps == 2 * seqs and HEADS % seqs == 0
+    body = head_split_device if split_heads else on_device
     return jax.shard_map(
-        on_device, mesh=mesh, in_specs=in_specs, out_specs=out_specs, check_vma=False
-    )
+        body, mesh=mesh, in_specs=in_specs, out_specs=out_specs, check_vma=False
+    )

time: 1060 us -> 460 us (0.43)
  waiting for transfers between devices: 722 us -> 147 us
  matrix products: 161 us -> 69.8 us
  starting transfers between devices: 1.21 us -> 41.1 us
  Pallas kernels: 0 us -> 27.6 us
  other arithmetic: 66.9 us -> 82.1 us
  between operations: 16.9 us -> 3.14 us
    psum x3 -> x0, waiting for transfers between devices: 369 us -> none  [the longest x2 248 us: on_device(): lax.psum((placed_attn, placed_up, placed_down), ('seq', 'rep'))]
    all_gather x7 -> x0, waiting for transfers between devices: 217 us -> none  [the longest x1 63.9 us: on_device(): lax.all_gather(attn_w.astype(lowered), 'rep', axis=2, tiled=True)]
    reduce_scatter x4 -> x0, waiting for transfers between devices: 136 us -> none  [the longest x1 76.2 us: on_device(): lax.psum_scatter(grad_attn_w.astype(jnp.bfloat16), 'seq', scatter_dimensi...]
    ppermute x0 -> x50, waiting for transfers between devices: none -> 131 us  [the longest x22 81 us: rep_swap(): return lax.ppermute(array, 'rep', [(i, i ^ bits) for i in range(size)])]
    dot_general x48 -> x31, matrix products: 158 us -> 69.5 us  [the longest x16 35.7 us: mm(): lax.dot_general(left, right, (((left_dim,), (right_dim,)), ((), ())), pre...]
    ppermute x0 -> x50, starting transfers between devices: none -> 31.9 us  [the longest x22 20.7 us: rep_swap(): return lax.ppermute(array, 'rep', [(i, i ^ bits) for i in range(size)])]
    pallas_call x0 -> x2, Pallas kernels: none -> 27.6 us  [the longest x1 16.7 us: attention_backward(): pl.pallas_call(functools.partial(attention_back_kernel, word_count, heads...]
    all_to_all x0 -> x2, waiting for transfers between devices: none -> 16.2 us  [the longest x1 8.39 us: head_split_device(): lax.all_to_all(grad_up.reshape(seq_count, part, hidden_part), 'seq', 0, 0)]
  transfers between devices with their start and end apart: 14 -> 52, of which waited for: 12 -> 30; matrix products, arithmetic and copies ran while one was open for 17% -> 27% of each run, Pallas kernels for 0% -> 2%
where the time goes in v1:
time: 460 us; the launch traced here: 454 us
  waiting for transfers between devices  147 us (32%)
  local copies, waits for them, and re-layouts  82.6 us (18%)
  other arithmetic  82.1 us (18%)
  matrix products  69.8 us (15%)
  starting transfers between devices  41.1 us (9%)
  Pallas kernels  27.6 us (6%)
    ppermute x22, waiting for transfers between devices, rep_swap(): return lax.ppermute(array, 'rep', [(i, i ^ bits) for i in range(size)])  81 us
    ppermute x26, waiting for transfers between devices, seq_swap(): return lax.ppermute(array, 'seq', [(i, i ^ bits) for i in range(size)])  50.2 us
    dot_general x16, matrix products, mm(): lax.dot_general(left, right, (((left_dim,), (right_dim,)), ((), ())), pre...  35.7 us
    unnamed x243, local copies, waits for them, and re-layouts  21.7 us
    ppermute x22, starting transfers between devices, rep_swap(): return lax.ppermute(array, 'rep', [(i, i ^ bits) for i in range(size)])  20.7 us
    pallas_call x1, Pallas kernels, attention_backward(): pl.pallas_call(functools.partial(attention_back_kernel, word_count, heads...  16.7 us
    convert_element_type x2, local copies, waits for them, and re-layouts, head_split_device(): grad_project.astype(jnp.float32)  12.8 us
    pallas_call x1, Pallas kernels, attention_forward(): pl.pallas_call(functools.partial(attention_kernel, word_count, heads), gr...  10.9 us
  transfers between devices with their start and end apart: 52, of which 30 were waited for; matrix products, arithmetic and copies ran while one was open for 27% of the time, Pallas kernels for 2%

profile of v1, /device:TPU:0, one launch (start us, length us, event | category | flops | bytes accessed | tf_op | source)
XLA Modules:
  0.0 453.7 jit_solution(10293430282834084519)
XLA Ops:
  3.5 2.8 multiply_sine_fusion
  8.1 2.5 collective-permute-start.1
  13.3 3.0 collective-permute-start.8
  18.3 17.4 %collective-permute-done.8 = bf16[96,192]{0,1:T(8,128)(2,1)S(1)} collective-permute-done((bf16[96,192]{0,1:T(8,128)(2,1)S(1)}, bf16[96,192]{0,1:T(8,128)(2,1)S(1)}, u32[]{:S(2)}, u32[]{:S(2)}) %collective-permute-start.8) | collective-permute-done | bytes 36896 | tf_op jit(solution)/shard_map/ppermute | solution.py:466
  35.9 4.9 %collective-permute-done.9 = bf16[2,96,192]{1,2,0:T(8,128)(2,1)S(1)} collective-permute-done((bf16[2,96,192]{1,2,0:T(8,128)(2,1)S(1)}, bf16[2,96,192]{1,2,0:T(8,128)(2,1)S(1)}, u32[]{:S(2)}, u32[]{:S(2)}) %collective-permute-start.9) | collective-permute-done | bytes 73760 | tf_op jit(solution)/shard_map/ppermute | solution.py:466
  47.8 2.5 collective-permute-start.4
  52.0 17.5 %collective-permute-done.4 = bf16[192,576]{0,1:T(8,128)(2,1)S(1)} collective-permute-done((bf16[192,576]{0,1:T(8,128)(2,1)S(1)}, bf16[192,576]{0,1:T(8,128)(2,1)S(1)}, u32[]{:S(2)}, u32[]{:S(2)}) %collective-permute-start.4) | collective-permute-done | bytes 221216 | tf_op jit(solution)/shard_map/ppermute | solution.py:466
  74.4 1.9 constant_dynamic-update-slice_fusion.18
  76.3 2.0 constant_dynamic-update-slice_fusion.17
  80.5 5.7 %collective-permute-done.5 = bf16[2,192,576]{2,1,0:T(8,128)(2,1)} collective-permute-done((bf16[2,192,576]{2,1,0:T(8,128)(2,1)}, bf16[2,192,576]{2,1,0:T(8,128)(2,1)}, u32[]{:S(2)}, u32[]{:S(2)}) %collective-permute-start.5) | collective-permute-done | bytes 442400 | tf_op jit(solution)/shard_map/ppermute | solution.py:466
  86.1 2.1 copy.170
  93.4 1.9 constant_dynamic-update-slice_fusion.16
  101.0 2.2 collective-permute-done.7
  103.2 2.1 copy.173
  109.7 3.3 reshape.1209
  118.2 10.9 %attention.1 = (f32[1152,192]{1,0:T(8,128)}, bf16[1152,192]{1,0:T(8,128)(2,1)}, f32[1152,128]{1,0:T(8,128)}) custom-call(bf16[1152,768]{1,0:T(8,128)(2,1)} %pad_maximum_fusion.query_ref.key_ref, bf16[1152,768]{1,0:T(8,128)(2,1)} %pad_maximum_fusion.query_ref.key_ref, f32[1,1152]{1,0:T(1,128)} %add_multiply_fusion.1.offset_ref), custom_call_target="tpu_custom_call" | custom-call | flops 1019215872 | bytes 5308416 | tf_op jit(solution)/shard_map/attention/pallas_call | solution.py:593
  139.1 2.6 collective-permute-done.19
  143.4 6.9 %collective-permute-done.25 = bf16[2,96,768]{2,1,0:T(8,128)(2,1)S(1)} collective-permute-done((bf16[2,96,768]{2,1,0:T(8,128)(2,1)}, bf16[2,96,768]{2,1,0:T(8,128)(2,1)S(1)}, u32[]{:S(2)}, u32[]{:S(2)}) %collective-permute-start.25) | collective-permute-done | bytes 294944 | tf_op jit(solution)/shard_map/ppermute | solution.py:466
  152.6 3.3 collective-permute-done.21
  157.8 7.3 %collective-permute-done.15 = bf16[288,768]{1,0:T(8,128)(2,1)S(1)} collective-permute-done((bf16[288,768]{1,0:T(8,128)(2,1)S(1)}, bf16[288,768]{1,0:T(8,128)(2,1)S(1)}, u32[]{:S(2)}, u32[]{:S(2)}) %collective-permute-start.15) | collective-permute-done | bytes 442400 | tf_op jit(solution)/shard_map/ppermute | solution.py:461
  167.0 11.2 %multiply_convert_fusion = (bf16[1152,768]{1,0:T(8,128)(2,1)S(1)}, f32[1152,768]{1,0:T(8,128)}, f32[1152,768]{1,0:T(8,128)}) fusion(f32[768]{0:T(1024)S(1)} %dynamic_slice.16, bf16[1152,768]{1,0:T(8,128)(2,1)S(1)} %constant_dynamic-update-slice_fusion, bf16[768,768]{1,0:T(8,128)(2,1)S(1)} %bitcast.268), kind=kOutput, calls=%fused_computation.7 | convolution fusion | flops 1417347072 | bytes 11799552 | tf_op jit(solution)/shard_map/dot_general | solution.py:544
  186.2 9.7 %collective-permute-done.27 = bf16[288,768]{1,0:T(8,128)(2,1)S(1)} collective-permute-done((bf16[288,768]{1,0:T(8,128)(2,1)}, bf16[288,768]{1,0:T(8,128)(2,1)S(1)}, u32[]{:S(2)}, u32[]{:S(2)}) %collective-permute-start.27) | collective-permute-done | bytes 442400 | tf_op jit(solution)/shard_map/ppermute | solution.py:461
  202.5 9.9 %collective-permute-done.29 = bf16[288,768]{1,0:T(8,128)(2,1)S(1)} collective-permute-done((bf16[288,768]{1,0:T(8,128)(2,1)S(1)}, bf16[288,768]{1,0:T(8,128)(2,1)S(1)}, u32[]{:S(2)}, u32[]{:S(2)}) %collective-permute-start.29) | collective-permute-done | bytes 442400 | tf_op jit(solution)/shard_map/ppermute | solution.py:461
  214.3 2.5 fusion.88
  225.8 2.8 convolution_convert_fusion
  228.6 4.5 all-to-all-start.1
  233.7 2.8 convolution_bitcast_fusion.2
  236.5 2.0 collective-permute-done.32
  238.5 2.5 multiply_reduce_fusion.1
  242.8 8.4 %all-to-all-done.1 = bf16[4,192,768]{2,1,0:T(8,128)(2,1)} async-done(((bf16[4,192,768]{2,1,0:T(8,128)(2,1)}), bf16[4,192,768]{2,1,0:T(8,128)(2,1)}, u32[]{:S(2)}, u32[]{:S(2)}) %all-to-all-start.1) | async-done | bytes 1179680 | tf_op jit(solution)/shard_map/all_to_all | solution.py:814
  252.9 6.9 %collective-permute-done.34 = bf16[288,768]{1,0:T(8,128)(2,1)} collective-permute-done((bf16[288,768]{1,0:T(8,128)(2,1)S(1)}, bf16[288,768]{1,0:T(8,128)(2,1)}, u32[]{:S(2)}, u32[]{:S(2)}) %collective-permute-start.34) | collective-permute-done | bytes 442400 | tf_op jit(solution)/shard_map/ppermute | solution.py:461
  265.6 16.7 %attention_back.1 = (f32[1152,384]{1,0:T(8,128)}, f32[1152,192]{1,0:T(8,128)}, f32[1152,192]{1,0:T(8,128)}) custom-call(bf16[1152,768]{1,0:T(8,128)(2,1)} %pad_maximum_fusion.query_ref.key_ref, bf16[1152,768]{1,0:T(8,128)(2,1)} %pad_maximum_fusion.query_ref.key_ref, f32[1,1152]{1,0:T(1,128)} %add_multiply_fusion.1.offset_ref, ...), custom_call_target="tpu_custom_call" | custom-call | flops 2548039680 | bytes 14155776 | tf_op jit(solution)/shard_map/attention_back/pallas_call | solution.py:677
  282.4 3.1 broadcast_multiply_fusion
  291.4 4.7 %all-to-all-start = ((bf16[4,192,1152]{2,1,0:T(8,128)(2,1)}), bf16[4,192,1152]{2,1,0:T(8,128)(2,1)}, u32[]{:S(2)}, u32[]{:S(2)}) async-start(bf16[4,192,1152]{2,1,0:T(8,128)(2,1)} %pad_maximum_fusion.2), calls=%async_computation | async-start | bytes 3538944 | tf_op jit(solution)/shard_map/all_to_all | solution.py:846
  296.2 3.7 convolution_bitcast_fusion.3
  301.3 2.6 fusion.118
  306.6 3.1 fusion.119
  310.5 7.8 %all-to-all-done = bf16[4,192,1152]{2,1,0:T(8,128)(2,1)} async-done(((bf16[4,192,1152]{2,1,0:T(8,128)(2,1)}), bf16[4,192,1152]{2,1,0:T(8,128)(2,1)}, u32[]{:S(2)}, u32[]{:S(2)}) %all-to-all-start) | async-done | bytes 1769504 | tf_op jit(solution)/shard_map/all_to_all | solution.py:846
  318.3 4.0 copy.184
  322.3 4.4 convert_bitcast_fusion
  326.8 6.8 %copy.185 = f32[6,192,4,192]{3,2,1,0:T(4,128)} copy(f32[6,192,4,192]{1,3,0,2:T(8,128)} %convert_bitcast_fusion) | data formatting | bytes 7077888 | tf_op jit(solution)/shard_map/convert_element_type | solution.py:874
  333.5 6.0 %reshape.1223 = f32[6,192,768]{2,1,0:T(8,128)} reshape(f32[6,192,4,192]{3,2,1,0:T(4,128)} %copy.185) | data formatting | bytes 7077888 | tf_op jit(solution)/shard_map/convert_element_type | solution.py:874
  339.6 6.9 %convolution_bitcast_fusion.1 = f32[8,7,192]{2,0,1:T(8,128)S(1)} fusion(f32[7,768,8]{1,2,0:T(8,128)S(1)} %copy-done, f32[1,192,768]{2,1,0:T(8,128)S(1)} %convolution_bitcast_fusion, f32[6,192,768]{2,1,0:T(8,128)} %reshape.1223, f32[1,7,192,768]{3,2,1,0:T(8,128)} %param.36), kind=kOutput, calls=%fused_computation.56 | convolution fusion | flops 101154816 | bytes 8472576 | tf_op jit(solution)/shard_map/jcg,jgr->jrc/dot_general | solution.py:877
  352.5 2.2 collective-permute-done.38
  355.9 2.0 pad_maximum_fusion.13
  357.9 2.1 collective-permute-done.39
  360.1 2.6 fusion.103
  362.7 3.1 collective-permute-done.40
  372.7 7.0 %custom-call.8 = f32[9,8,8]{2,1,0:T(8,128)S(1)} custom-call(f32[9,8,8]{2,1,0:T(8,128)S(1)} %fusion.63), custom_call_target="Cholesky" | custom-call | tf_op jit(solution)/shard_map/jit(cholesky)/cholesky | solution.py:902
  379.9 5.6 %custom-call.9 = f32[9,1,8,8]{2,3,1,0:T(8,128)S(1)} custom-call(f32[9,1,8,8]{3,2,1,0:T(8,128)S(1)} %select_bitcast_fusion), custom_call_target="InvertDiagBlocksLowerTriangular" | custom-call | tf_op jit(solution)/shard_map/jit(_solve_triangular)/vmap()/triangular_solve | solution.py:903
  386.5 3.3 fusion.86
  391.0 4.5 fusion.87
  399.4 3.2 collective-permute-done.44
  405.1 2.0 collective-permute-done.45
  407.9 3.8 collective-permute-done.46
  412.0 5.5 %collective-permute-done.47 = f32[8,2688]{1,0:T(8,128)S(1)} collective-permute-done((f32[8,2688]{1,0:T(8,128)S(1)}, f32[8,2688]{1,0:T(8,128)S(1)}, u32[]{:S(2)}, u32[]{:S(2)}) %collective-permute-start.47) | collective-permute-done | bytes 86048 | tf_op jit(solution)/shard_map/ppermute | solution.py:466
  418.7 3.4 collective-permute-done.48
  423.6 3.5 fusion.65
  427.1 3.4 fusion.51
  431.9 3.2 copy.196
  435.1 4.2 subtract_bitcast_fusion.1
  441.2 3.5 fusion.122
  444.8 2.8 subtract_bitcast_fusion
  447.6 1.9 multiply_subtract_fusion.1
  (523 shorter events, 142.0 us)
Async XLA Ops:
  0.7 338.9 %copy-start = (f32[7,768,8]{1,2,0:T(8,128)S(1)}, f32[7,768,8]{1,2,0:T(8,128)}, u32[]{:S(2)}) copy-start(f32[7,768,8]{1,2,0:T(8,128)} %param.39) | copy-start | bytes 516100
  7.6 65.1 %collective-permute-start = (bf16[304,768]{1,0:T(8,128)(2,1)}, bf16[304,768]{1,0:T(8,128)(2,1)}, u32[]{:S(2)}, u32[]{:S(2)}) collective-permute-start(bf16[304,768]{1,0:T(8,128)(2,1)} %pad_maximum_fusion.16), channel_id=1, source_target_pairs={{0,8},{8,0},{16,24},{24,16},{1,9},{9,1},{17,25},{25,17},{2,10},{10... | collective-permute-start | bytes 1400840 | tf_op jit(solution)/shard_map/ppermute | solution.py:461
  8.1 66.2 %collective-permute-start.1 = (bf16[304,768]{1,0:T(8,128)(2,1)}, bf16[304,768]{1,0:T(8,128)(2,1)}, u32[]{:S(2)}, u32[]{:S(2)}) collective-permute-start(bf16[304,768]{1,0:T(8,128)(2,1)} %pad_maximum_fusion.16), channel_id=1, source_target_pairs={{0,16},{8,24},{16,0},{24,8},{1,17},{9,25},{17,1},{25,9},{2,18},{10... | collective-permute-start | bytes 1400840 | tf_op jit(solution)/shard_map/ppermute | solution.py:461
  11.6 36.1 %collective-permute-start.3 = (bf16[192,576]{0,1:T(8,128)(2,1)}, bf16[192,576]{0,1:T(8,128)(2,1)S(1)}, u32[]{:S(2)}, u32[]{:S(2)}) collective-permute-start(bf16[192,576]{0,1:T(8,128)(2,1)} %bitcast.287), channel_id=1, source_target_pairs={{0,0},{1,1},{2,8},{3,9},{4,16},{5,17},{6,24},{7,25},{8,2},{9,3},{1... | collective-permute-start | bytes 663560 | tf_op jit(solution)/shard_map/ppermute | solution.py:475
  13.3 22.5 %collective-permute-start.8 = (bf16[96,192]{0,1:T(8,128)(2,1)S(1)}, bf16[96,192]{0,1:T(8,128)(2,1)S(1)}, u32[]{:S(2)}, u32[]{:S(2)}) collective-permute-start(bf16[96,192]{0,1:T(8,128)(2,1)S(1)} %get-tuple-element.132), channel_id=1, source_target_pairs={{0,4},{1,5},{2,6},{3,7},{4,0},{5,1},{6,2},{7,3},{8,12},{9,13},{10,... | collective-permute-start | bytes 110600 | tf_op jit(solution)/shard_map/ppermute | solution.py:466
  16.3 26.2 %collective-permute-start.22 = (bf16[96,768]{1,0:T(8,128)(2,1)S(1)}, bf16[96,768]{1,0:T(8,128)(2,1)S(1)}, u32[]{:S(2)}, u32[]{:S(2)}) collective-permute-start(bf16[96,768]{1,0:T(8,128)(2,1)S(1)} %get-tuple-element.135), channel_id=1, source_target_pairs={{0,4},{1,5},{2,6},{3,7},{4,0},{5,1},{6,2},{7,3},{8,12},{9,13},{10,... | collective-permute-start | bytes 442376 | tf_op jit(solution)/shard_map/ppermute | solution.py:466
  35.8 5.1 %collective-permute-start.9 = (bf16[2,96,192]{1,2,0:T(8,128)(2,1)S(1)}, bf16[2,96,192]{1,2,0:T(8,128)(2,1)S(1)}, u32[]{:S(2)}, u32[]{:S(2)}) collective-permute-start(bf16[2,96,192]{1,2,0:T(8,128)(2,1)S(1)} %maximum_select_fusion.19), channel_id=1, source_target_pairs={{0,2},{1,3},{2,0},{3,1},{4,6},{5,7},{6,4},{7,5},{8,10},{9,11},{10,... | collective-permute-start | bytes 221192 | tf_op jit(solution)/shard_map/ppermute | solution.py:466
  40.9 5.2 %collective-permute-start.10 = (bf16[2,96,192]{1,2,0:T(8,128)(2,1)S(1)}, bf16[2,96,192]{1,2,0:T(8,128)(2,1)S(1)}, u32[]{:S(2)}, u32[]{:S(2)}) collective-permute-start(bf16[2,96,192]{1,2,0:T(8,128)(2,1)S(1)} %maximum_select_fusion.19), channel_id=1, source_target_pairs={{0,1},{1,0},{2,3},{3,2},{4,5},{5,4},{6,7},{7,6},{8,9},{9,8},{10,11... | collective-permute-start | bytes 221192 | tf_op jit(solution)/shard_map/ppermute | solution.py:466
  42.5 5.1 %collective-permute-start.11 = (bf16[2,96,192]{1,2,0:T(8,128)(2,1)S(1)}, bf16[2,96,192]{1,2,0:T(8,128)(2,1)S(1)}, u32[]{:S(2)}, u32[]{:S(2)}) collective-permute-start(bf16[2,96,192]{1,2,0:T(8,128)(2,1)S(1)} %collective-permute-done.9), channel_id=1, source_target_pairs={{0,1},{1,0},{2,3},{3,2},{4,5},{5,4},{6,7},{7,6},{8,9},{9,8},{10,11... | collective-permute-start | bytes 221192 | tf_op jit(solution)/shard_map/ppermute | solution.py:466
  46.1 33.8 %collective-permute-start.17 = (bf16[192,384]{1,0:T(8,128)(2,1)S(1)}, bf16[192,384]{1,0:T(8,128)(2,1)}, u32[]{:S(2)}, u32[]{:S(2)}) collective-permute-start(bf16[192,384]{1,0:T(8,128)(2,1)S(1)} %convert_element_type.169), channel_id=1, source_target_pairs={{0,0},{1,1},{2,8},{3,9},{4,16},{5,17},{6,24},{7,25},{8,2},{9,3},{1... | collective-permute-start | bytes 442376 | tf_op jit(solution)/shard_map/ppermute | solution.py:475
  47.6 89.2 %collective-permute-start.23 = (bf16[2,96,768]{2,1,0:T(8,128)(2,1)}, bf16[2,96,768]{2,1,0:T(8,128)(2,1)}, u32[]{:S(2)}, u32[]{:S(2)}) collective-permute-start(bf16[2,96,768]{2,1,0:T(8,128)(2,1)} %maximum_select_fusion.14), channel_id=1, source_target_pairs={{0,2},{1,3},{2,0},{3,1},{4,6},{5,7},{6,4},{7,5},{8,10},{9,11},{10,... | collective-permute-start | bytes 884744 | tf_op jit(solution)/shard_map/ppermute | solution.py:466
  47.8 21.7 %collective-permute-start.4 = (bf16[192,576]{0,1:T(8,128)(2,1)S(1)}, bf16[192,576]{0,1:T(8,128)(2,1)S(1)}, u32[]{:S(2)}, u32[]{:S(2)}) collective-permute-start(bf16[192,576]{0,1:T(8,128)(2,1)S(1)} %collective-permute-done.3), channel_id=1, source_target_pairs={{0,4},{1,5},{2,6},{3,7},{4,0},{5,1},{6,2},{7,3},{8,12},{9,13},{10,... | collective-permute-start | bytes 663560 | tf_op jit(solution)/shard_map/ppermute | solution.py:466
  72.6 13.6 %collective-permute-start.5 = (bf16[2,192,576]{2,1,0:T(8,128)(2,1)}, bf16[2,192,576]{2,1,0:T(8,128)(2,1)}, u32[]{:S(2)}, u32[]{:S(2)}) collective-permute-start(bf16[2,192,576]{2,1,0:T(8,128)(2,1)} %copy.169), channel_id=1, source_target_pairs={{0,2},{1,3},{2,0},{3,1},{4,6},{5,7},{6,4},{7,5},{8,10},{9,11},{10,... | collective-permute-start | bytes 1327112 | tf_op jit(solution)/shard_map/ppermute | solution.py:466
  72.8 15.4 %collective-permute-start.6 = (bf16[2,192,576]{2,1,0:T(8,128)(2,1)}, bf16[2,192,576]{2,1,0:T(8,128)(2,1)S(1)}, u32[]{:S(2)}, u32[]{:S(2)}) collective-permute-start(bf16[2,192,576]{2,1,0:T(8,128)(2,1)} %copy.169), channel_id=1, source_target_pairs={{0,1},{1,0},{2,3},{3,2},{4,5},{5,4},{6,7},{7,6},{8,9},{9,8},{10,11... | collective-permute-start | bytes 1327112 | tf_op jit(solution)/shard_map/ppermute | solution.py:466
  74.4 18.2 %collective-permute-start.2 = (bf16[304,768]{1,0:T(8,128)(2,1)}, bf16[304,768]{1,0:T(8,128)(2,1)}, u32[]{:S(2)}, u32[]{:S(2)}) collective-permute-start(bf16[304,768]{1,0:T(8,128)(2,1)} %collective-permute-done.1), channel_id=1, source_target_pairs={{0,8},{8,0},{16,24},{24,16},{1,9},{9,1},{17,25},{25,17},{2,10},{10... | collective-permute-start | bytes 1400840 | tf_op jit(solution)/shard_map/ppermute | solution.py:461
  79.9 63.5 %collective-permute-start.24 = (bf16[2,96,768]{2,1,0:T(8,128)(2,1)}, bf16[2,96,768]{2,1,0:T(8,128)(2,1)}, u32[]{:S(2)}, u32[]{:S(2)}) collective-permute-start(bf16[2,96,768]{2,1,0:T(8,128)(2,1)} %maximum_select_fusion.14), channel_id=1, source_target_pairs={{0,1},{1,0},{2,3},{3,2},{4,5},{5,4},{6,7},{7,6},{8,9},{9,8},{10,11... | collective-permute-start | bytes 884744 | tf_op jit(solution)/shard_map/ppermute | solution.py:466
  86.1 45.0 %collective-permute-start.18 = (bf16[192,384]{1,0:T(8,128)(2,1)}, bf16[192,384]{1,0:T(8,128)(2,1)}, u32[]{:S(2)}, u32[]{:S(2)}) collective-permute-start(bf16[192,384]{1,0:T(8,128)(2,1)} %collective-permute-done.17), channel_id=1, source_target_pairs={{0,4},{1,5},{2,6},{3,7},{4,0},{5,1},{6,2},{7,3},{8,12},{9,13},{10,... | collective-permute-start | bytes 442376 | tf_op jit(solution)/shard_map/ppermute | solution.py:466
  88.2 15.0 %collective-permute-start.7 = (bf16[2,192,576]{2,1,0:T(8,128)(2,1)}, bf16[2,192,576]{2,1,0:T(8,128)(2,1)}, u32[]{:S(2)}, u32[]{:S(2)}) collective-permute-start(bf16[2,192,576]{2,1,0:T(8,128)(2,1)} %collective-permute-done.5), channel_id=1, source_target_pairs={{0,1},{1,0},{2,3},{3,2},{4,5},{5,4},{6,7},{7,6},{8,9},{9,8},{10,11... | collective-permute-start | bytes 1327112 | tf_op jit(solution)/shard_map/ppermute | solution.py:466
  96.0 20.3 %copy-start.81 = (bf16[32,768]{1,0:T(8,128)(2,1)}, bf16[32,768]{1,0:T(8,128)(2,1)S(1)}, u32[]{:S(2)}) copy-start(bf16[32,768]{1,0:T(8,128)(2,1)S(1)} %get-tuple-element.125) | copy-start | bytes 147460
  97.5 18.8 %copy-start.83 = (bf16[32,768]{1,0:T(8,128)(2,1)}, bf16[32,768]{1,0:T(8,128)(2,1)S(1)}, u32[]{:S(2)}) copy-start(bf16[32,768]{1,0:T(8,128)(2,1)S(1)} %get-tuple-element.117) | copy-start | bytes 147460
  131.0 7.7 %collective-permute-start.12 = (bf16[576,768]{1,0:T(8,128)(2,1)S(1)}, bf16[576,768]{1,0:T(8,128)(2,1)S(1)}, u32[]{:S(2)}, u32[]{:S(2)}) collective-permute-start(bf16[576,768]{1,0:T(8,128)(2,1)S(1)} %pad_maximum_fusion.9), channel_id=1, source_target_pairs={{0,8},{8,0},{16,24},{24,16},{1,9},{9,1},{17,25},{25,17},{2,10},{10... | collective-permute-start | bytes 2654216 | tf_op jit(solution)/shard_map/ppermute | solution.py:461
  132.3 9.5 %collective-permute-start.19 = (bf16[2,192,384]{2,1,0:T(8,128)(2,1)S(1)}, bf16[2,192,384]{2,1,0:T(8,128)(2,1)S(1)}, u32[]{:S(2)}, u32[]{:S(2)}) collective-permute-start(bf16[2,192,384]{2,1,0:T(8,128)(2,1)S(1)} %maximum_select_fusion.12), channel_id=1, source_target_pairs={{0,2},{1,3},{2,0},{3,1},{4,6},{5,7},{6,4},{7,5},{8,10},{9,11},{10,... | collective-permute-start | bytes 884744 | tf_op jit(solution)/shard_map/ppermute | solution.py:466
  134.1 18.5 %collective-permute-start.20 = (bf16[2,192,384]{2,1,0:T(8,128)(2,1)S(1)}, bf16[2,192,384]{2,1,0:T(8,128)(2,1)S(1)}, u32[]{:S(2)}, u32[]{:S(2)}) collective-permute-start(bf16[2,192,384]{2,1,0:T(8,128)(2,1)S(1)} %maximum_select_fusion.12), channel_id=1, source_target_pairs={{0,1},{1,0},{2,3},{3,2},{4,5},{5,4},{6,7},{7,6},{8,9},{9,8},{10,11... | collective-permute-start | bytes 884744 | tf_op jit(solution)/shard_map/ppermute | solution.py:466
  136.8 13.5 %collective-permute-start.25 = (bf16[2,96,768]{2,1,0:T(8,128)(2,1)}, bf16[2,96,768]{2,1,0:T(8,128)(2,1)S(1)}, u32[]{:S(2)}, u32[]{:S(2)}) collective-permute-start(bf16[2,96,768]{2,1,0:T(8,128)(2,1)} %collective-permute-done.23), channel_id=1, source_target_pairs={{0,1},{1,0},{2,3},{3,2},{4,5},{5,4},{6,7},{7,6},{8,9},{9,8},{10,11... | collective-permute-start | bytes 884744 | tf_op jit(solution)/shard_map/ppermute | solution.py:466
  139.0 12.6 %collective-permute-start.13 = (bf16[288,768]{1,0:T(8,128)(2,1)S(1)}, bf16[288,768]{1,0:T(8,128)(2,1)S(1)}, u32[]{:S(2)}, u32[]{:S(2)}) collective-permute-start(bf16[288,768]{1,0:T(8,128)(2,1)S(1)} %fusion.23), channel_id=1, source_target_pairs={{0,16},{8,24},{16,0},{24,8},{1,17},{9,25},{17,1},{25,9},{2,18},{10... | collective-permute-start | bytes 1327112 | tf_op jit(solution)/shard_map/ppermute | solution.py:461
  141.8 14.1 %collective-permute-start.21 = (bf16[2,192,384]{2,1,0:T(8,128)(2,1)S(1)}, bf16[2,192,384]{2,1,0:T(8,128)(2,1)S(1)}, u32[]{:S(2)}, u32[]{:S(2)}) collective-permute-start(bf16[2,192,384]{2,1,0:T(8,128)(2,1)S(1)} %collective-permute-done.19), channel_id=1, source_target_pairs={{0,1},{1,0},{2,3},{3,2},{4,5},{5,4},{6,7},{7,6},{8,9},{9,8},{10,11... | collective-permute-start | bytes 884744 | tf_op jit(solution)/shard_map/ppermute | solution.py:466
  151.6 26.6 %copy-start.33 = (bf16[2,2,2,96,768]{4,3,2,1,0:T(8,128)(2,1)}, bf16[2,2,2,96,768]{4,3,2,1,0:T(8,128)(2,1)S(1)}, u32[]{:S(2)}) copy-start(bf16[2,2,2,96,768]{4,3,2,1,0:T(8,128)(2,1)S(1)} %maximum_select_fusion.4) | copy-start | bytes 3538948
  152.4 12.7 %collective-permute-start.14 = (bf16[288,768]{1,0:T(8,128)(2,1)S(1)}, bf16[288,768]{1,0:T(8,128)(2,1)S(1)}, u32[]{:S(2)}, u32[]{:S(2)}) collective-permute-start(bf16[288,768]{1,0:T(8,128)(2,1)S(1)} %fusion.34), channel_id=1, source_target_pairs={{0,8},{8,0},{16,24},{24,16},{1,9},{9,1},{17,25},{25,17},{2,10},{10... | collective-permute-start | bytes 1327112 | tf_op jit(solution)/shard_map/ppermute | solution.py:461
  152.5 12.6 %collective-permute-start.15 = (bf16[288,768]{1,0:T(8,128)(2,1)S(1)}, bf16[288,768]{1,0:T(8,128)(2,1)S(1)}, u32[]{:S(2)}, u32[]{:S(2)}) collective-permute-start(bf16[288,768]{1,0:T(8,128)(2,1)S(1)} %fusion.34), channel_id=1, source_target_pairs={{0,16},{8,24},{16,0},{24,8},{1,17},{9,25},{17,1},{25,9},{2,18},{10... | collective-permute-start | bytes 1327112 | tf_op jit(solution)/shard_map/ppermute | solution.py:461
  165.1 1.8 collective-permute-start.16
  180.0 2.5 collective-permute-start.26
  183.5 12.4 %collective-permute-start.27 = (bf16[288,768]{1,0:T(8,128)(2,1)}, bf16[288,768]{1,0:T(8,128)(2,1)S(1)}, u32[]{:S(2)}, u32[]{:S(2)}) collective-permute-start(bf16[288,768]{1,0:T(8,128)(2,1)} %fusion.19), channel_id=1, source_target_pairs={{0,16},{8,24},{16,0},{24,8},{1,17},{9,25},{17,1},{25,9},{2,18},{10... | collective-permute-start | bytes 1327112 | tf_op jit(solution)/shard_map/ppermute | solution.py:461
  198.3 15.9 %copy-start.106 = (f32[1152,768]{1,0:T(8,128)S(1)}, f32[1152,768]{1,0:T(8,128)}, u32[]{:S(2)}) copy-start(f32[1152,768]{1,0:T(8,128)} %get-tuple-element.154) | copy-start | bytes 10616836
  199.7 14.6 %copy-start.105 = (f32[1152,768]{1,0:T(8,128)S(1)}, f32[1152,768]{1,0:T(8,128)}, u32[]{:S(2)}) copy-start(f32[1152,768]{1,0:T(8,128)} %get-tuple-element.68) | copy-start | bytes 10616836
  199.7 12.7 %collective-permute-start.28 = (bf16[288,768]{1,0:T(8,128)(2,1)S(1)}, bf16[288,768]{1,0:T(8,128)(2,1)S(1)}, u32[]{:S(2)}, u32[]{:S(2)}) collective-permute-start(bf16[288,768]{1,0:T(8,128)(2,1)S(1)} %convert_element_type.175), channel_id=1, source_target_pairs={{0,8},{8,0},{16,24},{24,16},{1,9},{9,1},{17,25},{25,17},{2,10},{10... | collective-permute-start | bytes 1327112 | tf_op jit(solution)/shard_map/ppermute | solution.py:461
  199.8 12.6 %collective-permute-start.29 = (bf16[288,768]{1,0:T(8,128)(2,1)S(1)}, bf16[288,768]{1,0:T(8,128)(2,1)S(1)}, u32[]{:S(2)}, u32[]{:S(2)}) collective-permute-start(bf16[288,768]{1,0:T(8,128)(2,1)S(1)} %convert_element_type.175), channel_id=1, source_target_pairs={{0,16},{8,24},{16,0},{24,8},{1,17},{9,25},{17,1},{25,9},{2,18},{10... | collective-permute-start | bytes 1327112 | tf_op jit(solution)/shard_map/ppermute | solution.py:461
  212.4 1.8 collective-permute-start.30
  218.6 4.3 collective-permute-start.31
  225.2 13.4 %collective-permute-start.32 = (bf16[288,768]{1,0:T(8,128)(2,1)}, bf16[288,768]{1,0:T(8,128)(2,1)}, u32[]{:S(2)}, u32[]{:S(2)}) collective-permute-start(bf16[288,768]{1,0:T(8,128)(2,1)} %fusion.16), channel_id=1, source_target_pairs={{0,16},{8,24},{16,0},{24,8},{1,17},{9,25},{17,1},{25,9},{2,18},{10... | collective-permute-start | bytes 1327112 | tf_op jit(solution)/shard_map/ppermute | solution.py:461
  228.6 22.5 %all-to-all-start.1 = ((bf16[4,192,768]{2,1,0:T(8,128)(2,1)}), bf16[4,192,768]{2,1,0:T(8,128)(2,1)}, u32[]{:S(2)}, u32[]{:S(2)}) async-start(bf16[4,192,768]{2,1,0:T(8,128)(2,1)} %bitcast.270), calls=%async_computation.1 | async-start | bytes 2359296 | tf_op jit(solution)/shard_map/all_to_all | solution.py:814
  242.3 17.5 %collective-permute-start.33 = (bf16[288,768]{1,0:T(8,128)(2,1)S(1)}, bf16[288,768]{1,0:T(8,128)(2,1)S(1)}, u32[]{:S(2)}, u32[]{:S(2)}) collective-permute-start(bf16[288,768]{1,0:T(8,128)(2,1)S(1)} %convert_element_type.180), channel_id=1, source_target_pairs={{0,8},{8,0},{16,24},{24,16},{1,9},{9,1},{17,25},{25,17},{2,10},{10... | collective-permute-start | bytes 1327112 | tf_op jit(solution)/shard_map/ppermute | solution.py:461
  242.4 17.4 %collective-permute-start.34 = (bf16[288,768]{1,0:T(8,128)(2,1)S(1)}, bf16[288,768]{1,0:T(8,128)(2,1)}, u32[]{:S(2)}, u32[]{:S(2)}) collective-permute-start(bf16[288,768]{1,0:T(8,128)(2,1)S(1)} %convert_element_type.180), channel_id=1, source_target_pairs={{0,16},{8,24},{16,0},{24,8},{1,17},{9,25},{17,1},{25,9},{2,18},{10... | collective-permute-start | bytes 1327112 | tf_op jit(solution)/shard_map/ppermute | solution.py:461
  259.9 2.0 collective-permute-start.35
  285.4 15.8 %copy-start.17 = (bf16[1152,384]{1,0:T(8,128)(2,1)}, bf16[1152,384]{1,0:T(8,128)(2,1)S(1)}, u32[]{:S(2)}) copy-start(bf16[1152,384]{1,0:T(8,128)(2,1)S(1)} %get-tuple-element.86) | copy-start | bytes 2654212
  291.4 26.9 %all-to-all-start = ((bf16[4,192,1152]{2,1,0:T(8,128)(2,1)}), bf16[4,192,1152]{2,1,0:T(8,128)(2,1)}, u32[]{:S(2)}, u32[]{:S(2)}) async-start(bf16[4,192,1152]{2,1,0:T(8,128)(2,1)} %pad_maximum_fusion.2), calls=%async_computation | async-start | bytes 3538944 | tf_op jit(solution)/shard_map/all_to_all | solution.py:846
  350.1 4.6 %collective-permute-start.38 = (f32[8,2304]{1,0:T(8,128)}, f32[8,2304]{1,0:T(8,128)S(1)}, u32[]{:S(2)}, u32[]{:S(2)}) collective-permute-start(f32[8,2304]{1,0:T(8,128)} %concatenate.380), channel_id=1, source_target_pairs={{0,1},{1,0},{2,3},{3,2},{4,5},{5,4},{6,7},{7,6},{8,9},{9,8},{10,11... | collective-permute-start | bytes 221192 | tf_op jit(solution)/shard_map/ppermute | solution.py:466
  355.6 4.4 collective-permute-start.39
  357.9 37.8 %collective-permute-start.36 = (bf16[576,768]{1,0:T(8,128)(2,1)}, bf16[576,768]{1,0:T(8,128)(2,1)}, u32[]{:S(2)}, u32[]{:S(2)}) collective-permute-start(bf16[576,768]{1,0:T(8,128)(2,1)} %pad_maximum_fusion.13), channel_id=1, source_target_pairs={{0,8},{8,0},{16,24},{24,16},{1,9},{9,1},{17,25},{25,17},{2,10},{10... | collective-permute-start | bytes 2654216 | tf_op jit(solution)/shard_map/ppermute | solution.py:461
  360.0 5.8 %collective-permute-start.40 = (f32[8,2304]{1,0:T(8,128)S(1)}, f32[8,2304]{1,0:T(8,128)S(1)}, u32[]{:S(2)}, u32[]{:S(2)}) collective-permute-start(f32[8,2304]{1,0:T(8,128)S(1)} %add.321), channel_id=1, source_target_pairs={{0,4},{1,5},{2,6},{3,7},{4,0},{5,1},{6,2},{7,3},{8,12},{9,13},{10,... | collective-permute-start | bytes 221192 | tf_op jit(solution)/shard_map/ppermute | solution.py:466
  365.9 14.0 %copy-start.98 = (pred[8,8]{1,0:T(8,128)(4,1)S(1)}, pred[8,8]{1,0:T(8,128)(4,1)}, u32[]{:S(2)}) copy-start(pred[8,8]{1,0:T(8,128)(4,1)} %iota_compare_fusion.3) | copy-start | bytes 196
  365.9 19.7 %copy-start.90 = (f32[8,8]{1,0:T(8,128)S(1)}, f32[8,8]{1,0:T(8,128)}, u32[]{:S(2)}) copy-start(f32[8,8]{1,0:T(8,128)} %fusion.75) | copy-start | bytes 772
  366.6 2.0 collective-permute-start.41
  368.6 4.0 collective-permute-start.42
  386.1 41.0 %copy-start.80 = (f32[8,192]{1,0:T(8,128)}, f32[8,192]{1,0:T(8,128)S(1)}, u32[]{:S(2)}) copy-start(f32[8,192]{1,0:T(8,128)S(1)} %fusion.71) | copy-start | bytes 18436
  386.3 37.4 %copy-start.70 = (f32[8,768]{1,0:T(8,128)}, f32[8,768]{1,0:T(8,128)S(1)}, u32[]{:S(2)}) copy-start(f32[8,768]{1,0:T(8,128)S(1)} %fusion.67) | copy-start | bytes 73732
  386.5 54.7 %copy-start.69 = (f32[7,8,192]{2,1,0:T(8,128)}, f32[7,8,192]{2,1,0:T(8,128)S(1)}, u32[]{:S(2)}) copy-start(f32[7,8,192]{2,1,0:T(8,128)S(1)} %fusion.53) | copy-start | bytes 129028
  395.5 1.5 collective-permute-start.43
  397.1 5.5 %collective-permute-start.44 = (f32[8,2688]{1,0:T(8,128)S(1)}, f32[8,2688]{1,0:T(8,128)S(1)}, u32[]{:S(2)}, u32[]{:S(2)}) collective-permute-start(f32[8,2688]{1,0:T(8,128)S(1)} %slice_select_fusion), channel_id=1, source_target_pairs={{0,16},{8,24},{16,0},{24,8},{1,17},{9,25},{17,1},{25,9},{2,18},{10... | collective-permute-start | bytes 258056 | tf_op jit(solution)/shard_map/ppermute | solution.py:461
  397.9 13.9 %collective-permute-start.37 = (bf16[288,768]{1,0:T(8,128)(2,1)S(1)}, bf16[288,768]{1,0:T(8,128)(2,1)S(1)}, u32[]{:S(2)}, u32[]{:S(2)}) collective-permute-start(bf16[288,768]{1,0:T(8,128)(2,1)S(1)} %fusion.13), channel_id=1, source_target_pairs={{0,16},{8,24},{16,0},{24,8},{1,17},{9,25},{17,1},{25,9},{2,18},{10... | collective-permute-start | bytes 1327112 | tf_op jit(solution)/shard_map/ppermute | solution.py:461
  402.6 4.6 %collective-permute-start.45 = (f32[8,2688]{1,0:T(8,128)S(1)}, f32[8,2688]{1,0:T(8,128)S(1)}, u32[]{:S(2)}, u32[]{:S(2)}) collective-permute-start(f32[8,2688]{1,0:T(8,128)S(1)} %select_add_fusion.1), channel_id=1, source_target_pairs={{0,1},{1,0},{2,3},{3,2},{4,5},{5,4},{6,7},{7,6},{8,9},{9,8},{10,11... | collective-permute-start | bytes 258056 | tf_op jit(solution)/shard_map/ppermute | solution.py:466
  407.2 4.6 %collective-permute-start.46 = (f32[8,2688]{1,0:T(8,128)S(1)}, f32[8,2688]{1,0:T(8,128)S(1)}, u32[]{:S(2)}, u32[]{:S(2)}) collective-permute-start(f32[8,2688]{1,0:T(8,128)S(1)} %add.330), channel_id=1, source_target_pairs={{0,2},{1,3},{2,0},{3,1},{4,6},{5,7},{6,4},{7,5},{8,10},{9,11},{10,... | collective-permute-start | bytes 258056 | tf_op jit(solution)/shard_map/ppermute | solution.py:466
  411.7 5.8 %collective-permute-start.47 = (f32[8,2688]{1,0:T(8,128)S(1)}, f32[8,2688]{1,0:T(8,128)S(1)}, u32[]{:S(2)}, u32[]{:S(2)}) collective-permute-start(f32[8,2688]{1,0:T(8,128)S(1)} %add.331), channel_id=1, source_target_pairs={{0,4},{1,5},{2,6},{3,7},{4,0},{5,1},{6,2},{7,3},{8,12},{9,13},{10,... | collective-permute-start | bytes 258056 | tf_op jit(solution)/shard_map/ppermute | solution.py:466
  417.6 4.6 %collective-permute-start.48 = (f32[8,2688]{1,0:T(8,128)S(1)}, f32[8,2688]{1,0:T(8,128)S(1)}, u32[]{:S(2)}, u32[]{:S(2)}) collective-permute-start(f32[8,2688]{1,0:T(8,128)S(1)} %add.332), channel_id=1, source_target_pairs={{0,16},{8,24},{16,0},{24,8},{1,17},{9,25},{17,1},{25,9},{2,18},{10... | collective-permute-start | bytes 258056 | tf_op jit(solution)/shard_map/ppermute | solution.py:461
  422.1 1.5 collective-permute-start.49
  (95 other events, 390.9 us)
